TPU v7x, 32 devices: a whole 2x2x4 slice. The times are simulated.
32 devices in a mesh: row: 4 (over y, x), col: 8 (over z, core).
Axes of the slice: x: 2, y: 2, z: 4, core: 2. Of those that a mesh axis runs over, the one named last changes fastest.
Arguments:
- messages: bfloat16 [4, 8, 1024, 512], P('row', 'col'), may hold values from -6 to 6
- targets: int32 [4, 8, 1024], P('row', 'col'), may hold values from 0 to 255
- reverse_rows: int32 [4, 8, 8, 128], P('row', 'col'), may hold values from 0 to 127, as said below
- nodes: bfloat16 [8, 256, 512], P('col', 'row'), may hold values from -6 to 6
- w_in: bfloat16 [2, 1536, 512], replicated, may hold values from -0.15625 to 0.15625
- w_res: bfloat16 [2, 2, 2, 512, 512], replicated, may hold values from -0.25 to 0.25
- w_node: bfloat16 [2, 512, 512], replicated, may hold values from -0.25 to 0.25
Outputs:
- edge_out: bfloat16 [4, 8, 1024, 512], P('row', 'col')
- node_out: bfloat16 [8, 256, 512], P('col', 'row')
Inputs may be any that keep to these rules, and one draw needn't show every extreme that they name: reverse_rows[s, c, k] is a permutation of the block's rows, and the reversal is an involution: the reversed edge of the reversed edge is the edge itself.
All inputs are finite; a program needn't handle non-finite values.
Results may differ from a plain program's by a relative error of at most 0.0065.
Values may be sent and summed in bfloat16 or wider, within the bound.
No kernel may reach another device: no remote copies, remote signals or barrier semaphores. Data moves between devices by JAX's collectives and lax.ppermute only.
A program may use at most 64 MiB of HBM per device.

v0:
```python
import functools
import math

import jax
import jax.numpy as jnp
from jax import lax
from jax.experimental import pallas as pl
from jax.experimental.pallas import tpu as pltpu
from jax.sharding import PartitionSpec as P


OFFSETS = (0, 0, 1, -1, 2, -2, 3, -3)
ROOT_HALF = 0.7071067811865476
PAIRS = len(OFFSETS) // 2
F32 = jnp.float32
BF16 = jnp.bfloat16


def dot(a, b):
    return jnp.dot(a, b, preferred_element_type=F32)


def silu(v):
    half = 0.5 * v
    return half + half * jnp.tanh(half)


def call(body, outs, args, flops, spaces={}, out_space=pltpu.VMEM, scratch=(), limit=32 << 20, aliases={}):
    moved = sum(math.prod(a.shape) * a.dtype.itemsize for a in list(args) + list(outs))
    return pl.pallas_call(
        body,
        out_shape=tuple(jax.ShapeDtypeStruct(o.shape, o.dtype) for o in outs),
        in_specs=[
            pl.BlockSpec(memory_space=spaces.get(i, pltpu.VMEM)) for i in range(len(args))
        ],
        out_specs=tuple(pl.BlockSpec(memory_space=out_space) for _ in outs),
        scratch_shapes=list(scratch),
        input_output_aliases=aliases,
        compiler_params=pltpu.CompilerParams(vmem_limit_bytes=limit),
        cost_estimate=pl.CostEstimate(flops=flops, bytes_accessed=moved, transcendentals=0),
    )(*args)


def partner_numbers(targets, me, share):
    return ((targets // share) ^ me) * share + targets % share


def hot_rows(targets, first, count):
    points = lax.broadcasted_iota(jnp.int32, (count, targets.shape[1]), 0) + first
    return (points == targets).astype(F32).astype(BF16)


def joined(refs):
    if len(refs) == 1:
        return refs[0][...]
    return jnp.concatenate([ref[...] for ref in refs], axis=0)


def placed(order_ref, k):
    block = order_ref.shape[1]
    place = lax.broadcasted_iota(jnp.int32, (block, block), 0)
    return (place == order_ref[k : k + 1, :]).astype(F32).astype(BF16)


def split_columns(total, outs):
    at = 0
    for exact, sent in zip(outs[::2], outs[1::2]):
        piece = total[:, at : at + exact.shape[1]]
        exact[...] = piece
        sent[...] = piece.astype(BF16)
        at += exact.shape[1]


def partial_body(targets_ref, m_ref, *outs):
    split_columns(sums_of(targets_ref, 0, m_ref[...], outs[0].shape[0]), outs)


def swapped(ref, bit, share):
    count = ref.shape[0] // share
    parts = [ref[(k ^ bit) * share : (k ^ bit) * share + share, :] for k in range(count)]
    return jnp.concatenate(parts, axis=0).astype(F32)


def add_body(bits, share, *refs):
    count = len(bits)
    for p, bit in enumerate(bits):
        total = refs[p][...] + swapped(refs[count + p], bit, share)
        refs[2 * count + 2 * p][...] = total
        refs[2 * count + 2 * p + 1][...] = total.astype(BF16)


def update_body(bits, share, scale, w_ref, *refs):
    count = len(bits)
    nodes, table_ref = refs[2 * count : -1], refs[-1]
    totals = [refs[p][...] + swapped(refs[count + p], bit, share) for p, bit in enumerate(bits)]
    z = (jnp.concatenate(totals, axis=1) * scale).astype(BF16)
    table_ref[...] = (joined(nodes).astype(F32) + silu(dot(z, w_ref[...]))).astype(BF16)


def order_body(order_ref, hot_ref, out):
    block = order_ref.shape[1]
    for k in range(out.shape[0] // block):
        rows = pl.ds(k * block, block)
        out[rows, :] = dot(placed(order_ref, k), hot_ref[rows, :]).astype(BF16)


def pre_body(layer, order_ref, *refs):
    (w_ref, w_node_ref, out, w_node_out), at = refs[-4:], 0
    w_node_out[...] = w_node_ref[layer]
    block = order_ref.shape[1]
    for ref in refs[:-4]:
        rows = min(ref.shape[0], out.shape[0] - at)
        width = ref.shape[1]
        m_rows = [
            dot(placed(order_ref, (at + i) // block), ref[i : i + block, :]).astype(BF16)
            for i in range(0, rows, block)
        ]
        out[at : at + rows, :] = dot(jnp.concatenate(m_rows, axis=0), w_ref[layer, :width, :])
        at += rows


def sent_rows(k, block, hot_ref, pre_ref, table, w):
    rows = pl.ds(k * block, block)
    h_rows = dot(hot_ref[rows, :], table).astype(BF16)
    return (pre_ref[rows, :] + dot(h_rows, w)).astype(BF16)


def send_body(layer, first, hot_ref, pre_ref, w_ref, table_ref, *outs):
    block, width = outs[0].shape
    table = table_ref[...]
    w = w_ref[layer, width : 2 * width, :]
    for half, out in enumerate(outs):
        out[...] = sent_rows(first + half, block, hot_ref, pre_ref, table, w)


def edge_blocks(layer, got, m_blocks, w_ref):
    x1 = [silu(g).astype(BF16) for g in got]
    a1 = [silu(dot(x, w_ref[layer, 0, 0])).astype(BF16) for x in x1]
    x2 = [
        ((x.astype(F32) + silu(dot(a, w_ref[layer, 0, 1]))) * ROOT_HALF).astype(BF16)
        for x, a in zip(x1, a1)
    ]
    a2 = [silu(dot(x, w_ref[layer, 1, 0])).astype(BF16) for x in x2]
    for old, x, a in zip(m_blocks, x2, a2):
        x3 = (x.astype(F32) + silu(dot(a, w_ref[layer, 1, 1]))) * ROOT_HALF
        yield ((old.astype(F32) + x3) * ROOT_HALF).astype(BF16)


def sums_of(targets_ref, first, new, points):
    return dot(hot_rows(targets_ref[:, first : first + new.shape[0]], 0, points), new)


def local_body(layer, last, hot_ref, sent_ref, pre_ref, table_ref, m_ref, w_in_ref, w_ref, *refs):
    part_ref, new_ref, third_ref = refs[-3:]
    width, local = m_ref.shape[1], new_ref.shape[0]
    block = local // 2
    table = table_ref[...]
    w_mid, w_end = w_in_ref[layer, width : 2 * width, :], w_in_ref[layer, 2 * width :, :]
    got, old = [], []
    for k in range(2):
        rows = slice(k * block, (k + 1) * block)
        h_tgt = dot(hot_ref[rows, :], table).astype(BF16)
        received = sent_rows(k ^ 1, block, sent_ref, pre_ref, table, w_mid)
        got.append(received.astype(F32) + dot(h_tgt, w_end))
        old.append(m_ref[rows, :])
    for k, new in enumerate(edge_blocks(layer, got, old, w_ref)):
        new_ref[k * block : (k + 1) * block, :] = new
    h_tgt = dot(hot_ref[local:, :], table).astype(BF16)
    part_ref[...] = dot(h_tgt, w_end)
    if last:
        third_ref[...] = table_ref[: third_ref.shape[0], :]
    else:
        third_ref[...] = sums_of(refs[0], 0, new_ref[...], third_ref.shape[0])


def new_rows(layer, m_at, part_at, part_ref, m_ref, w_ref, got_refs):
    got, old = [], []
    for i, ref in enumerate(got_refs):
        size = ref.shape[0]
        rows = slice(part_at + i * size, part_at + (i + 1) * size)
        got.append(ref[...].astype(F32) + part_ref[rows, :])
        old.append(m_ref[m_at + i * size : m_at + (i + 1) * size, :])
    return edge_blocks(layer, got, old, w_ref)


def edge_body(
    layer, at, first, part_at, count, part_ref, m_ref, w_ref, targets_ref, sum_ref, *refs
):
    got, new_ref, sums = refs[:count], refs[count], refs[count + 1 :]
    size = got[0].shape[0]
    for i, new in enumerate(new_rows(layer, at, part_at, part_ref, m_ref, w_ref, got)):
        new_ref[i * size : (i + 1) * size, :] = new
    total = sum_ref[...] + sums_of(targets_ref, first, new_ref[...], sum_ref.shape[0])
    if len(sums) == 1:
        sums[0][...] = total
    else:
        split_columns(total, sums)


def last_body(layer, at, first, part_at, count, part_ref, m_ref, w_ref, *refs):
    got, done_ref = refs[:count], refs[count]
    out, rows_ref, sems = refs[-3:]
    size = got[0].shape[0]
    copies = []
    if len(done_ref.shape) == 2 and done_ref.shape[0] == first:
        copies.append(pltpu.make_async_copy(done_ref, out.at[pl.ds(0, first), :], sems.at[count]))
        copies[0].start()
    for i, new in enumerate(new_rows(layer, at, part_at, part_ref, m_ref, w_ref, got)):
        rows = pl.ds(i * size, size)
        rows_ref[rows, :] = new
        target = out.at[pl.ds(first + i * size, size), :]
        copies.append(pltpu.make_async_copy(rows_ref.at[rows, :], target, sems.at[i]))
        copies[-1].start()
    for copy in copies:
        copy.wait()


def row_move(value, bit):
    count = lax.axis_size("row")
    return lax.ppermute(value, "row", [(s, s ^ bit) for s in range(count)])


def col_shift(value, steps):
    count = lax.axis_size("col")
    return lax.ppermute(value, "col", [(s, (s + steps) % count) for s in range(count)])


def column_pieces(width, count):
    lanes = width // 128
    sizes = [lanes // count + (p < lanes % count) for p in range(count)]
    return [128 * size for size in sizes]


def sds(rows, width, dtype):
    return jax.ShapeDtypeStruct((rows, width), dtype)


def shards(messages, targets, reverse_rows, nodes, w_in, w_res, w_node):
    m = messages[0, 0]
    order = reverse_rows[0, 0]
    share_h = nodes[0]
    edges, width = m.shape
    share = share_h.shape[0]
    blocks, block = order.shape
    pair_rows = 2 * block
    count = lax.axis_size("row")
    assert count & (count - 1) == 0
    points = count * share
    scale = 1.0 / math.sqrt(edges // share)
    me = lax.axis_index("row").astype(jnp.int32)
    layers = w_in.shape[0]
    product = 2 * pair_rows * width * width
    rounds = count.bit_length() - 1
    pieces = column_pieces(width, rounds)
    piece_shapes = [sds(points, piece, t) for piece in pieces for t in (F32, BF16)]
    own = partner_numbers(targets[0], me, share)
    table = [share_h]
    sums = call(partial_body, piece_shapes, (own, m), 2 * points * edges * width)
    for k in range(1, count):
        table.append(row_move(share_h, k))
    hot = (own[0][:, None] == jnp.arange(points, dtype=jnp.int32)[None, :]).astype(BF16)
    groups = (tuple(range(2, blocks - 2)), tuple(range(blocks - 2, blocks)))
    m_parts = [(m, 0)] + [(m, ks[0] * block) for ks in groups]
    for layer in range(layers):
        first, last = layer == 0, layer == layers - 1
        for r in range(rounds):
            bits = [1 << ((p + r) % rounds) for p in range(rounds)]
            got = []
            for p, bit in enumerate(bits):
                got.append(row_move(sums[2 * p + 1], bit))
            if r < rounds - 1:
                sums = call(
                    functools.partial(add_body, bits, share),
                    piece_shapes,
                    (*sums[::2], *got),
                    points * width,
                )
        if first:
            (hot_sent,) = call(
                order_body,
                [sds(edges, points, BF16)],
                (order, hot),
                2 * edges * block * points,
            )
        pre, w_point = call(
            functools.partial(pre_body, layer),
            [sds(edges, width, F32), sds(width, width, BF16)],
            (order, *((m,) if first else [part for part, _ in m_parts]), w_in, w_node),
            PAIRS * product,
        )
        (h,) = call(
            functools.partial(update_body, bits, share, scale),
            [sds(points, width, BF16)],
            (w_point, *sums[::2], *got, *table),
            2 * points * width * width,
        )
        table = [h]
        sent = {}
        for pair in (2, 1, 3):
            outs = call(
                functools.partial(send_body, layer, 2 * pair),
                [sds(block, width, BF16)] * 2,
                (hot_sent, pre, w_in, h),
                2 * product,
            )
            for half, out in enumerate(outs):
                k = 2 * pair + half
                sent[k ^ 1] = col_shift(out, OFFSETS[k])
        out = call(
            functools.partial(local_body, layer, last),
            [sds(edges - pair_rows, width, F32), sds(pair_rows, width, BF16)]
            + [sds(share, width, BF16) if last else sds(points, width, F32)],
            (hot, hot_sent, pre, h, m_parts[0][0], w_in, w_res) + (() if last else (own,)),
            12 * product,
        )
        part, done, sums = out[0], [out[1]], [out[2]]
        if last:
            share_h = out[2]
        for name, ks, (source, at) in zip(("near", "far"), groups, m_parts[1:]):
            where = (layer, at, ks[0] * block, ks[0] * block - pair_rows, len(ks))
            got = [sent[k] for k in ks]
            if last:
                done = call(
                    functools.partial(last_body, *where),
                    [sds(edges, width, BF16)],
                    (part, source, w_res, *got, *done),
                    2 * len(ks) * product,
                    spaces={3 + len(ks): pltpu.HBM} if name == "far" else {},
                    out_space=pltpu.HBM,
                    scratch=(
                        pltpu.VMEM((len(ks) * block, width), BF16),
                        pltpu.SemaphoreType.DMA((len(ks) + 1,)),
                    ),
                    aliases={3 + len(ks): 0} if name == "far" else {},
                )
            else:
                new, *sums = call(
                    functools.partial(edge_body, *where),
                    [sds(len(ks) * block, width, BF16)]
                    + (piece_shapes if name == "far" else [sds(points, width, F32)]),
                    (part, source, w_res, own, *sums, *got),
                    3 * len(ks) * product,
                )
                done.append(new)
        m_parts = [(new, 0) for new in done]
    return (done[0][None, None], share_h[None])


def solution(mesh):
    in_specs = (
        P("row", "col", None, None),
        P("row", "col", None),
        P("row", "col", None, None),
        P("col", "row", None),
        P(),
        P(),
        P(),
    )
    out_specs = (P("row", "col", None, None), P("col", "row", None))
    return jax.shard_map(shards, mesh=mesh, in_specs=in_specs, out_specs=out_specs, check_vma=False)
```

profile of v0, /device:TPU:1, one launch (start us, length us, event | category | flops | bytes accessed | tf_op | source)
XLA Modules:
  0.0 78.9 jit_solution(13260872135751223893)
XLA Ops:
  0.6 3.0 %collective-permute-start.6 = (bf16[64,512]{1,0:T(8,128)(2,1)}, bf16[64,512]{1,0:T(8,128)(2,1)S(1)}, u32[]{:S(2)}, u32[]{:S(2)}) collective-permute-start(bf16[64,512]{1,0:T(8,128)(2,1)} %bitcast.24), channel_id=1, source_target_pairs={{0,24},{8,16},{16,8},{24,0},{1,25},{9,17},{17,9},{25,1},{2,26},{10... | collective-permute-start | bytes 196616 | tf_op jit(solution)/shard_map/ppermute | solution.py:220
  3.7 0.2 collective-permute-start.5
  3.9 0.1 collective-permute-start.4
  4.1 0.7 fusion.1.targets_ref.refs_0_
  4.8 0.0 copy-start.2
  4.8 1.2 %copy-done.2 = bf16[1,1,1024,512]{3,2,1,0:T(8,128)(2,1)S(1)} copy-done((bf16[1,1,1024,512]{3,2,1,0:T(8,128)(2,1)S(1)}, bf16[1,1,1024,512]{3,2,1,0:T(8,128)(2,1)}, u32[]{:S(2)}) %copy-start.2) | copy-done | bytes 1048600
  6.0 0.4 shard_map.88
  6.4 1.4 %collective-permute-start = (bf16[256,256]{1,0:T(8,128)(2,1)S(1)}, bf16[256,256]{1,0:T(8,128)(2,1)S(1)}, u32[]{:S(2)}, u32[]{:S(2)}) collective-permute-start(bf16[256,256]{1,0:T(8,128)(2,1)S(1)} %get-tuple-element.47), channel_id=1, source_target_pairs={{0,8},{8,0},{16,24},{24,16},{1,9},{9,1},{17,25},{25,17},{2,10},{10... | collective-permute-start | bytes 393224 | tf_op jit(solution)/shard_map/ppermute | solution.py:220
  7.8 1.2 %collective-permute-start.1 = (bf16[256,256]{1,0:T(8,128)(2,1)S(1)}, bf16[256,256]{1,0:T(8,128)(2,1)S(1)}, u32[]{:S(2)}, u32[]{:S(2)}) collective-permute-start(bf16[256,256]{1,0:T(8,128)(2,1)S(1)} %get-tuple-element.48), channel_id=1, source_target_pairs={{0,16},{8,24},{16,0},{24,8},{1,17},{9,25},{17,1},{25,9},{2,18},{10... | collective-permute-start | bytes 393224 | tf_op jit(solution)/shard_map/ppermute | solution.py:220
  9.1 0.7 fusion.4
  9.8 0.6 collective-permute-done.refs_2_
  10.3 1.6 %collective-permute-done.1.refs_3_ = bf16[256,256]{1,0:T(8,128)(2,1)S(1)} collective-permute-done((bf16[256,256]{1,0:T(8,128)(2,1)S(1)}, bf16[256,256]{1,0:T(8,128)(2,1)S(1)}, u32[]{:S(2)}, u32[]{:S(2)}) %collective-permute-start.1) | collective-permute-done | bytes 131104 | tf_op jit(solution)/shard_map/ppermute | solution.py:220
  12.0 0.1 shard_map.89
  12.0 1.3 %collective-permute-start.2 = (bf16[256,256]{1,0:T(8,128)(2,1)S(1)}, bf16[256,256]{1,0:T(8,128)(2,1)S(1)}, u32[]{:S(2)}, u32[]{:S(2)}) collective-permute-start(bf16[256,256]{1,0:T(8,128)(2,1)S(1)} %get-tuple-element.51), channel_id=1, source_target_pairs={{0,16},{8,24},{16,0},{24,8},{1,17},{9,25},{17,1},{25,9},{2,18},{10... | collective-permute-start | bytes 393224 | tf_op jit(solution)/shard_map/ppermute | solution.py:220
  13.3 0.0 collective-permute-start.3
  13.3 0.2 fusion.hot_ref
  13.5 0.0 copy-start.7
  13.6 0.7 copy-done.7
  14.2 0.3 shard_map.86.sent_ref.hot_ref
  14.5 0.0 copy-start.3
  14.5 1.2 %copy-done.3 = bf16[1,1,1024,512]{3,2,1,0:T(8,128)(2,1)S(1)} copy-done((bf16[1,1,1024,512]{3,2,1,0:T(8,128)(2,1)S(1)}, bf16[1,1,1024,512]{3,2,1,0:T(8,128)(2,1)}, u32[]{:S(2)}) %copy-start.3) | copy-done | bytes 1048600
  15.8 1.2 %copy-done.4 = bf16[2,512,512]{2,1,0:T(8,128)(2,1)S(1)} copy-done((bf16[2,512,512]{2,1,0:T(8,128)(2,1)S(1)}, bf16[2,512,512]{2,1,0:T(8,128)(2,1)}, u32[]{:S(2)}) %copy-start.4) | copy-done | bytes 1048600
  17.0 1.0 %shard_map.87 = (f32[1024,512]{1,0:T(8,128)S(1)}, bf16[512,512]{1,0:T(8,128)(2,1)S(1)}) custom-call(s32[8,128]{1,0:T(8,128)S(1)} %bitcast.29, bf16[1024,512]{1,0:T(8,128)(2,1)S(1)} %bitcast.20, bf16[2,1536,512]{2,1,0:T(8,128)(2,1)S(1)} %copy-done, bf16[2,512,512]{2,1,0:T(8,128)(2,1)S(1)} %copy-done.4), custom_call_target="tpu_custom_call" | custom-call | flops 536870912 | bytes 7868416 | tf_op jit(solution)/shard_map/pallas_call | solution.py:30
  18.0 0.0 collective-permute-done.4.refs_5_
  18.0 0.4 shard_map.90.table_ref.refs_4_
  18.4 0.6 shard_map.95
  19.0 0.6 shard_map.93
  19.6 0.0 copy-start.1
  19.6 0.6 shard_map.92
  20.2 6.7 %collective-permute-start.11 = (bf16[128,512]{1,0:T(8,128)(2,1)S(1)}, bf16[128,512]{1,0:T(8,128)(2,1)S(1)}, u32[]{:S(2)}, u32[]{:S(2)}) collective-permute-start(bf16[128,512]{1,0:T(8,128)(2,1)S(1)} %get-tuple-element.62), channel_id=1, source_target_pairs={{0,5},{1,6},{2,7},{3,0},{4,1},{5,2},{6,3},{7,4},{8,13},{9,14},{10,... | collective-permute-start | bytes 393224 | tf_op jit(solution)/shard_map/ppermute | solution.py:225
  26.9 0.2 collective-permute-start.9
  27.1 1.3 %collective-permute-start.10 = (bf16[128,512]{1,0:T(8,128)(2,1)S(1)}, bf16[128,512]{1,0:T(8,128)(2,1)S(1)}, u32[]{:S(2)}, u32[]{:S(2)}) collective-permute-start(bf16[128,512]{1,0:T(8,128)(2,1)S(1)} %get-tuple-element.59), channel_id=1, source_target_pairs={{0,2},{1,3},{2,4},{3,5},{4,6},{5,7},{6,0},{7,1},{8,10},{9,11},{10,... | collective-permute-start | bytes 393224 | tf_op jit(solution)/shard_map/ppermute | solution.py:225
  28.4 0.0 collective-permute-start.7
  28.4 1.7 %collective-permute-start.8 = (bf16[128,512]{1,0:T(8,128)(2,1)S(1)}, bf16[128,512]{1,0:T(8,128)(2,1)S(1)}, u32[]{:S(2)}, u32[]{:S(2)}) collective-permute-start(bf16[128,512]{1,0:T(8,128)(2,1)S(1)} %get-tuple-element.57), channel_id=1, source_target_pairs={{0,1},{1,2},{2,3},{3,4},{4,5},{5,6},{6,7},{7,0},{8,9},{9,10},{10,1... | collective-permute-start | bytes 393224 | tf_op jit(solution)/shard_map/ppermute | solution.py:225
  30.1 2.4 %shard_map.91 = (f32[768,512]{1,0:T(8,128)S(1)}, bf16[256,512]{1,0:T(8,128)(2,1)S(1)}, f32[256,512]{1,0:T(8,128)S(1)}) custom-call(bf16[1024,256]{1,0:T(8,128)(2,1)S(1)} %fusion.hot_ref, bf16[1024,256]{1,0:T(8,128)(2,1)S(1)} %shard_map.86.sent_ref.hot_ref, f32[1024,512]{1,0:T(8,128)S(1)} %get-tuple-element.43.pre_ref, ...), custom_call_target="tpu_custom_call" | custom-call | flops 1610612736 | bytes 14159872 | tf_op jit(solution)/shard_map/pallas_call | solution.py:30
  32.5 4.5 %collective-permute-start.12 = (bf16[128,512]{1,0:T(8,128)(2,1)S(1)}, bf16[128,512]{1,0:T(8,128)(2,1)S(1)}, u32[]{:S(2)}, u32[]{:S(2)}) collective-permute-start(bf16[128,512]{1,0:T(8,128)(2,1)S(1)} %get-tuple-element.63), channel_id=1, source_target_pairs={{0,3},{1,4},{2,5},{3,6},{4,7},{5,0},{6,1},{7,2},{8,11},{9,12},{10,... | collective-permute-start | bytes 393224 | tf_op jit(solution)/shard_map/ppermute | solution.py:225
  37.0 0.0 collective-permute-done.10.refs_3_
  37.0 0.3 collective-permute-done.8.refs_1_
  37.3 2.2 %shard_map.94 = (bf16[512,512]{1,0:T(8,128)(2,1)S(1)}, f32[256,512]{1,0:T(8,128)S(1)}) custom-call(f32[768,512]{1,0:T(8,128)S(1)} %get-tuple-element.54.part_ref, bf16[1024,512]{1,0:T(8,128)(2,1)S(1)} %bitcast.22, bf16[2,2,2,512,512]{4,3,2,1,0:T(8,128)(2,1)S(1)} %copy-done.1, s32[1,1024]{1,0:T(1,128)S(1)} %fusion.1.targets_ref.refs_0_, ...), custom_call_target="tpu_custom_call" | custom-call | flops 1610612736 | bytes 8916992 | tf_op jit(solution)/shard_map/pallas_call | solution.py:30
  39.5 1.2 %collective-permute-done.12.refs_1_ = bf16[128,512]{1,0:T(8,128)(2,1)S(1)} collective-permute-done((bf16[128,512]{1,0:T(8,128)(2,1)S(1)}, bf16[128,512]{1,0:T(8,128)(2,1)S(1)}, u32[]{:S(2)}, u32[]{:S(2)}) %collective-permute-start.12) | collective-permute-done | bytes 131104 | tf_op jit(solution)/shard_map/ppermute | solution.py:225
  40.7 1.4 %shard_map.96 = (bf16[256,512]{1,0:T(8,128)(2,1)S(1)}, f32[256,256]{1,0:T(8,128)S(1)}, bf16[256,256]{1,0:T(8,128)(2,1)S(1)}, f32[256,256]{1,0:T(8,128)S(1)}, bf16[256,256]{1,0:T(8,128)(2,1)S(1)}) custom-call(f32[768,512]{1,0:T(8,128)S(1)} %get-tuple-element.54.part_ref, bf16[1024,512]{1,0:T(8,128)(2,1)S(1)} %bitcast.23, ...), custom_call_target="tpu_custom_call" | custom-call | flops 805306368 | bytes 8654848 | tf_op jit(solution)/shard_map/pallas_call | solution.py:30
  42.1 1.3 %collective-permute-start.13 = (bf16[256,256]{1,0:T(8,128)(2,1)S(1)}, bf16[256,256]{1,0:T(8,128)(2,1)S(1)}, u32[]{:S(2)}, u32[]{:S(2)}) collective-permute-start(bf16[256,256]{1,0:T(8,128)(2,1)S(1)} %get-tuple-element.69), channel_id=1, source_target_pairs={{0,8},{8,0},{16,24},{24,16},{1,9},{9,1},{17,25},{25,17},{2,10},{10... | collective-permute-start | bytes 393224 | tf_op jit(solution)/shard_map/ppermute | solution.py:220
  43.3 0.2 collective-permute-start.14
  43.6 2.4 %collective-permute-done.13.refs_2_ = bf16[256,256]{1,0:T(8,128)(2,1)S(1)} collective-permute-done((bf16[256,256]{1,0:T(8,128)(2,1)S(1)}, bf16[256,256]{1,0:T(8,128)(2,1)S(1)}, u32[]{:S(2)}, u32[]{:S(2)}) %collective-permute-start.13) | collective-permute-done | bytes 131104 | tf_op jit(solution)/shard_map/ppermute | solution.py:220
  45.9 1.2 %collective-permute-done.14.refs_3_ = bf16[256,256]{1,0:T(8,128)(2,1)S(1)} collective-permute-done((bf16[256,256]{1,0:T(8,128)(2,1)S(1)}, bf16[256,256]{1,0:T(8,128)(2,1)S(1)}, u32[]{:S(2)}, u32[]{:S(2)}) %collective-permute-start.14) | collective-permute-done | bytes 131104 | tf_op jit(solution)/shard_map/ppermute | solution.py:220
  47.1 0.1 shard_map.98
  47.2 0.3 collective-permute-start.15
  47.5 0.3 collective-permute-start.16
  47.8 1.1 %shard_map.97 = (f32[1024,512]{1,0:T(8,128)S(1)}, bf16[512,512]{1,0:T(8,128)(2,1)S(1)}) custom-call(s32[8,128]{1,0:T(8,128)S(1)} %bitcast.30, bf16[256,512]{1,0:T(8,128)(2,1)S(1)} %get-tuple-element.53.refs_0_.m_ref, bf16[512,512]{1,0:T(8,128)(2,1)S(1)} %get-tuple-element.60.refs_1_.m_ref, bf16[256,512]{1,0:T(8,128)(2,1)S(1)} %get-tuple-element.64.refs_2_.m_ref, ...), custom_call_target="tpu_custom_call" | custom-call | flops 536870912 | bytes 7868416 | tf_op jit(solution)/shard_map/pallas_call | solution.py:30
  48.9 3.4 %collective-permute-done.15.refs_2_ = bf16[256,256]{1,0:T(8,128)(2,1)S(1)} collective-permute-done((bf16[256,256]{1,0:T(8,128)(2,1)S(1)}, bf16[256,256]{1,0:T(8,128)(2,1)S(1)}, u32[]{:S(2)}, u32[]{:S(2)}) %collective-permute-start.15) | collective-permute-done | bytes 131104 | tf_op jit(solution)/shard_map/ppermute | solution.py:220
  52.3 0.4 shard_map.99.table_ref
  52.7 0.6 shard_map.103
  53.2 1.8 %collective-permute-start.21 = (bf16[128,512]{1,0:T(8,128)(2,1)S(1)}, bf16[128,512]{1,0:T(8,128)(2,1)S(1)}, u32[]{:S(2)}, u32[]{:S(2)}) collective-permute-start(bf16[128,512]{1,0:T(8,128)(2,1)S(1)} %get-tuple-element.80), channel_id=1, source_target_pairs={{0,6},{1,7},{2,0},{3,1},{4,2},{5,3},{6,4},{7,5},{8,14},{9,15},{10,... | collective-permute-start | bytes 393224 | tf_op jit(solution)/shard_map/ppermute | solution.py:225
  55.0 4.2 %collective-permute-start.22 = (bf16[128,512]{1,0:T(8,128)(2,1)S(1)}, bf16[128,512]{1,0:T(8,128)(2,1)S(1)}, u32[]{:S(2)}, u32[]{:S(2)}) collective-permute-start(bf16[128,512]{1,0:T(8,128)(2,1)S(1)} %get-tuple-element.81), channel_id=1, source_target_pairs={{0,2},{1,3},{2,4},{3,5},{4,6},{5,7},{6,0},{7,1},{8,10},{9,11},{10,... | collective-permute-start | bytes 393224 | tf_op jit(solution)/shard_map/ppermute | solution.py:225
  59.2 0.6 shard_map.102
  59.8 2.7 %collective-permute-start.19 = (bf16[128,512]{1,0:T(8,128)(2,1)S(1)}, bf16[128,512]{1,0:T(8,128)(2,1)S(1)}, u32[]{:S(2)}, u32[]{:S(2)}) collective-permute-start(bf16[128,512]{1,0:T(8,128)(2,1)S(1)} %get-tuple-element.78), channel_id=1, source_target_pairs={{0,7},{1,0},{2,1},{3,2},{4,3},{5,4},{6,5},{7,6},{8,15},{9,8},{10,9... | collective-permute-start | bytes 393224 | tf_op jit(solution)/shard_map/ppermute | solution.py:225
  62.4 0.6 shard_map.101
  63.0 2.1 %collective-permute-start.17 = (bf16[128,512]{1,0:T(8,128)(2,1)S(1)}, bf16[128,512]{1,0:T(8,128)(2,1)S(1)}, u32[]{:S(2)}, u32[]{:S(2)}) collective-permute-start(bf16[128,512]{1,0:T(8,128)(2,1)S(1)} %get-tuple-element.76), channel_id=1, source_target_pairs={{0,5},{1,6},{2,7},{3,0},{4,1},{5,2},{6,3},{7,4},{8,13},{9,14},{10,... | collective-permute-start | bytes 393224 | tf_op jit(solution)/shard_map/ppermute | solution.py:225
  65.2 0.6 collective-permute-start.18
  65.7 2.9 %shard_map.100 = (f32[768,512]{1,0:T(8,128)S(1)}, bf16[256,512]{1,0:T(8,128)(2,1)S(1)}, bf16[64,512]{1,0:T(8,128)(2,1)}) custom-call(bf16[1024,256]{1,0:T(8,128)(2,1)S(1)} %fusion.hot_ref, bf16[1024,256]{1,0:T(8,128)(2,1)S(1)} %shard_map.86.sent_ref.hot_ref, f32[1024,512]{1,0:T(8,128)S(1)} %get-tuple-element.65.pre_ref, ...), custom_call_target="tpu_custom_call" | custom-call | flops 1610612736 | bytes 12910592 | tf_op jit(solution)/shard_map/pallas_call | solution.py:30
  68.6 0.2 collective-permute-done.19.refs_0_
  68.8 2.7 %shard_map.104.refs_2_ = bf16[1024,512]{1,0:T(8,128)(2,1)} custom-call(f32[768,512]{1,0:T(8,128)S(1)} %get-tuple-element.75.part_ref, bf16[512,512]{1,0:T(8,128)(2,1)S(1)} %get-tuple-element.60.refs_1_.m_ref, bf16[2,2,2,512,512]{4,3,2,1,0:T(8,128)(2,1)S(1)} %copy-done.1, bf16[128,512]{1,0:T(8,128)(2,1)S(1)} %collective-permute-done.19.refs_0_, ...), custom_call_target="tpu_custom_call" | custom-call | flops 1073741824 | bytes 8126464 | tf_op jit(solution)/shard_map/pallas_call | solution.py:30
  71.5 5.4 %collective-permute-done.17.refs_0_ = bf16[128,512]{1,0:T(8,128)(2,1)S(1)} collective-permute-done((bf16[128,512]{1,0:T(8,128)(2,1)S(1)}, bf16[128,512]{1,0:T(8,128)(2,1)S(1)}, u32[]{:S(2)}, u32[]{:S(2)}) %collective-permute-start.17) | collective-permute-done | bytes 131104 | tf_op jit(solution)/shard_map/ppermute | solution.py:225
  76.9 1.8 %shard_map.105 = bf16[1024,512]{1,0:T(8,128)(2,1)} custom-call(f32[768,512]{1,0:T(8,128)S(1)} %get-tuple-element.75.part_ref, bf16[256,512]{1,0:T(8,128)(2,1)S(1)} %get-tuple-element.64.refs_2_.m_ref, bf16[2,2,2,512,512]{4,3,2,1,0:T(8,128)(2,1)S(1)} %copy-done.1, ...), custom_call_target="tpu_custom_call", output_to_operand_aliasing={{}: (5, {})} | custom-call | flops 536870912 | bytes 8388608 | tf_op jit(solution)/shard_map/pallas_call | solution.py:30
  (23 shorter events, 0.1 us)
Async XLA Ops:
  0.6 13.9 %copy-start = (bf16[2,1536,512]{2,1,0:T(8,128)(2,1)S(1)}, bf16[2,1536,512]{2,1,0:T(8,128)(2,1)}, u32[]{:S(2)}) copy-start(bf16[2,1536,512]{2,1,0:T(8,128)(2,1)} %w_ref.21) | copy-start | bytes 9437188
  0.6 17.4 %collective-permute-start.6 = (bf16[64,512]{1,0:T(8,128)(2,1)}, bf16[64,512]{1,0:T(8,128)(2,1)S(1)}, u32[]{:S(2)}, u32[]{:S(2)}) collective-permute-start(bf16[64,512]{1,0:T(8,128)(2,1)} %bitcast.24), channel_id=1, source_target_pairs={{0,24},{8,16},{16,8},{24,0},{1,25},{9,17},{17,9},{25,1},{2,26},{10... | collective-permute-start | bytes 196616 | tf_op jit(solution)/shard_map/ppermute | solution.py:220
  3.7 14.3 %collective-permute-start.5 = (bf16[64,512]{1,0:T(8,128)(2,1)}, bf16[64,512]{1,0:T(8,128)(2,1)S(1)}, u32[]{:S(2)}, u32[]{:S(2)}) collective-permute-start(bf16[64,512]{1,0:T(8,128)(2,1)} %bitcast.25), channel_id=1, source_target_pairs={{0,16},{8,24},{16,0},{24,8},{1,17},{9,25},{17,1},{25,9},{2,18},{10... | collective-permute-start | bytes 196616 | tf_op jit(solution)/shard_map/ppermute | solution.py:220
  3.9 14.1 %collective-permute-start.4 = (bf16[64,512]{1,0:T(8,128)(2,1)}, bf16[64,512]{1,0:T(8,128)(2,1)S(1)}, u32[]{:S(2)}, u32[]{:S(2)}) collective-permute-start(bf16[64,512]{1,0:T(8,128)(2,1)} %bitcast.26), channel_id=1, source_target_pairs={{0,8},{8,0},{16,24},{24,16},{1,9},{9,1},{17,25},{25,17},{2,10},{10... | collective-permute-start | bytes 196616 | tf_op jit(solution)/shard_map/ppermute | solution.py:220
  4.8 1.2 %copy-start.2 = (bf16[1,1,1024,512]{3,2,1,0:T(8,128)(2,1)S(1)}, bf16[1,1,1024,512]{3,2,1,0:T(8,128)(2,1)}, u32[]{:S(2)}) copy-start(bf16[1,1,1024,512]{3,2,1,0:T(8,128)(2,1)} %param.7) | copy-start | bytes 3145732
  6.4 3.9 %collective-permute-start = (bf16[256,256]{1,0:T(8,128)(2,1)S(1)}, bf16[256,256]{1,0:T(8,128)(2,1)S(1)}, u32[]{:S(2)}, u32[]{:S(2)}) collective-permute-start(bf16[256,256]{1,0:T(8,128)(2,1)S(1)} %get-tuple-element.47), channel_id=1, source_target_pairs={{0,8},{8,0},{16,24},{24,16},{1,9},{9,1},{17,25},{25,17},{2,10},{10... | collective-permute-start | bytes 393224 | tf_op jit(solution)/shard_map/ppermute | solution.py:220
  7.8 4.1 %collective-permute-start.1 = (bf16[256,256]{1,0:T(8,128)(2,1)S(1)}, bf16[256,256]{1,0:T(8,128)(2,1)S(1)}, u32[]{:S(2)}, u32[]{:S(2)}) collective-permute-start(bf16[256,256]{1,0:T(8,128)(2,1)S(1)} %get-tuple-element.48), channel_id=1, source_target_pairs={{0,16},{8,24},{16,0},{24,8},{1,17},{9,25},{17,1},{25,9},{2,18},{10... | collective-permute-start | bytes 393224 | tf_op jit(solution)/shard_map/ppermute | solution.py:220
  12.0 6.0 %collective-permute-start.2 = (bf16[256,256]{1,0:T(8,128)(2,1)S(1)}, bf16[256,256]{1,0:T(8,128)(2,1)S(1)}, u32[]{:S(2)}, u32[]{:S(2)}) collective-permute-start(bf16[256,256]{1,0:T(8,128)(2,1)S(1)} %get-tuple-element.51), channel_id=1, source_target_pairs={{0,16},{8,24},{16,0},{24,8},{1,17},{9,25},{17,1},{25,9},{2,18},{10... | collective-permute-start | bytes 393224 | tf_op jit(solution)/shard_map/ppermute | solution.py:220
  13.3 4.7 %collective-permute-start.3 = (bf16[256,256]{1,0:T(8,128)(2,1)S(1)}, bf16[256,256]{1,0:T(8,128)(2,1)S(1)}, u32[]{:S(2)}, u32[]{:S(2)}) collective-permute-start(bf16[256,256]{1,0:T(8,128)(2,1)S(1)} %get-tuple-element.52), channel_id=1, source_target_pairs={{0,8},{8,0},{16,24},{24,16},{1,9},{9,1},{17,25},{25,17},{2,10},{10... | collective-permute-start | bytes 393224 | tf_op jit(solution)/shard_map/ppermute | solution.py:220
  13.5 0.7 copy-start.7
  14.5 1.2 %copy-start.3 = (bf16[1,1,1024,512]{3,2,1,0:T(8,128)(2,1)S(1)}, bf16[1,1,1024,512]{3,2,1,0:T(8,128)(2,1)}, u32[]{:S(2)}) copy-start(bf16[1,1,1024,512]{3,2,1,0:T(8,128)(2,1)} %param.7) | copy-start | bytes 3145732
  15.8 1.2 %copy-start.4 = (bf16[2,512,512]{2,1,0:T(8,128)(2,1)S(1)}, bf16[2,512,512]{2,1,0:T(8,128)(2,1)}, u32[]{:S(2)}) copy-start(bf16[2,512,512]{2,1,0:T(8,128)(2,1)} %refs_4_.1) | copy-start | bytes 3145732
  17.0 1.1 %copy-start.6 = (bf16[1,64,512]{2,1,0:T(8,128)(2,1)S(1)}, bf16[1,64,512]{2,1,0:T(8,128)(2,1)}, u32[]{:S(2)}) copy-start(bf16[1,64,512]{2,1,0:T(8,128)(2,1)} %param.10) | copy-start | bytes 196612
  19.6 10.5 %copy-start.1 = (bf16[2,2,2,512,512]{4,3,2,1,0:T(8,128)(2,1)S(1)}, bf16[2,2,2,512,512]{4,3,2,1,0:T(8,128)(2,1)}, u32[]{:S(2)}) copy-start(bf16[2,2,2,512,512]{4,3,2,1,0:T(8,128)(2,1)} %w_ref.23) | copy-start | bytes 12582916
  20.2 19.4 %collective-permute-start.11 = (bf16[128,512]{1,0:T(8,128)(2,1)S(1)}, bf16[128,512]{1,0:T(8,128)(2,1)S(1)}, u32[]{:S(2)}, u32[]{:S(2)}) collective-permute-start(bf16[128,512]{1,0:T(8,128)(2,1)S(1)} %get-tuple-element.62), channel_id=1, source_target_pairs={{0,5},{1,6},{2,7},{3,0},{4,1},{5,2},{6,3},{7,4},{8,13},{9,14},{10,... | collective-permute-start | bytes 393224 | tf_op jit(solution)/shard_map/ppermute | solution.py:225
  26.9 5.6 %collective-permute-start.9 = (bf16[128,512]{1,0:T(8,128)(2,1)S(1)}, bf16[128,512]{1,0:T(8,128)(2,1)S(1)}, u32[]{:S(2)}, u32[]{:S(2)}) collective-permute-start(bf16[128,512]{1,0:T(8,128)(2,1)S(1)} %get-tuple-element.58), channel_id=1, source_target_pairs={{0,6},{1,7},{2,0},{3,1},{4,2},{5,3},{6,4},{7,5},{8,14},{9,15},{10,... | collective-permute-start | bytes 393224 | tf_op jit(solution)/shard_map/ppermute | solution.py:225
  27.1 9.9 %collective-permute-start.10 = (bf16[128,512]{1,0:T(8,128)(2,1)S(1)}, bf16[128,512]{1,0:T(8,128)(2,1)S(1)}, u32[]{:S(2)}, u32[]{:S(2)}) collective-permute-start(bf16[128,512]{1,0:T(8,128)(2,1)S(1)} %get-tuple-element.59), channel_id=1, source_target_pairs={{0,2},{1,3},{2,4},{3,5},{4,6},{5,7},{6,0},{7,1},{8,10},{9,11},{10,... | collective-permute-start | bytes 393224 | tf_op jit(solution)/shard_map/ppermute | solution.py:225
  28.4 8.6 %collective-permute-start.7 = (bf16[128,512]{1,0:T(8,128)(2,1)S(1)}, bf16[128,512]{1,0:T(8,128)(2,1)S(1)}, u32[]{:S(2)}, u32[]{:S(2)}) collective-permute-start(bf16[128,512]{1,0:T(8,128)(2,1)S(1)} %get-tuple-element.56), channel_id=1, source_target_pairs={{0,7},{1,0},{2,1},{3,2},{4,3},{5,4},{6,5},{7,6},{8,15},{9,8},{10,9... | collective-permute-start | bytes 393224 | tf_op jit(solution)/shard_map/ppermute | solution.py:225
  28.4 8.9 %collective-permute-start.8 = (bf16[128,512]{1,0:T(8,128)(2,1)S(1)}, bf16[128,512]{1,0:T(8,128)(2,1)S(1)}, u32[]{:S(2)}, u32[]{:S(2)}) collective-permute-start(bf16[128,512]{1,0:T(8,128)(2,1)S(1)} %get-tuple-element.57), channel_id=1, source_target_pairs={{0,1},{1,2},{2,3},{3,4},{4,5},{5,6},{6,7},{7,0},{8,9},{9,10},{10,1... | collective-permute-start | bytes 393224 | tf_op jit(solution)/shard_map/ppermute | solution.py:225
  32.5 8.2 %collective-permute-start.12 = (bf16[128,512]{1,0:T(8,128)(2,1)S(1)}, bf16[128,512]{1,0:T(8,128)(2,1)S(1)}, u32[]{:S(2)}, u32[]{:S(2)}) collective-permute-start(bf16[128,512]{1,0:T(8,128)(2,1)S(1)} %get-tuple-element.63), channel_id=1, source_target_pairs={{0,3},{1,4},{2,5},{3,6},{4,7},{5,0},{6,1},{7,2},{8,11},{9,12},{10,... | collective-permute-start | bytes 393224 | tf_op jit(solution)/shard_map/ppermute | solution.py:225
  40.7 7.1 %copy-start.5 = (bf16[2,512,512]{2,1,0:T(8,128)(2,1)S(1)}, bf16[2,512,512]{2,1,0:T(8,128)(2,1)}, u32[]{:S(2)}) copy-start(bf16[2,512,512]{2,1,0:T(8,128)(2,1)} %refs_4_.1) | copy-start | bytes 3145732
  40.7 7.1 %copy-start.8 = (s32[1,1,8,128]{3,2,1,0:T(8,128)S(1)}, s32[1,1,8,128]{3,2,1,0:T(8,128)}, u32[]{:S(2)}) copy-start(s32[1,1,8,128]{3,2,1,0:T(8,128)} %param.9) | copy-start | bytes 12292
  42.1 3.9 %collective-permute-start.13 = (bf16[256,256]{1,0:T(8,128)(2,1)S(1)}, bf16[256,256]{1,0:T(8,128)(2,1)S(1)}, u32[]{:S(2)}, u32[]{:S(2)}) collective-permute-start(bf16[256,256]{1,0:T(8,128)(2,1)S(1)} %get-tuple-element.69), channel_id=1, source_target_pairs={{0,8},{8,0},{16,24},{24,16},{1,9},{9,1},{17,25},{25,17},{2,10},{10... | collective-permute-start | bytes 393224 | tf_op jit(solution)/shard_map/ppermute | solution.py:220
  43.3 3.8 %collective-permute-start.14 = (bf16[256,256]{1,0:T(8,128)(2,1)S(1)}, bf16[256,256]{1,0:T(8,128)(2,1)S(1)}, u32[]{:S(2)}, u32[]{:S(2)}) collective-permute-start(bf16[256,256]{1,0:T(8,128)(2,1)S(1)} %get-tuple-element.70), channel_id=1, source_target_pairs={{0,16},{8,24},{16,0},{24,8},{1,17},{9,25},{17,1},{25,9},{2,18},{10... | collective-permute-start | bytes 393224 | tf_op jit(solution)/shard_map/ppermute | solution.py:220
  47.2 5.1 %collective-permute-start.15 = (bf16[256,256]{1,0:T(8,128)(2,1)S(1)}, bf16[256,256]{1,0:T(8,128)(2,1)S(1)}, u32[]{:S(2)}, u32[]{:S(2)}) collective-permute-start(bf16[256,256]{1,0:T(8,128)(2,1)S(1)} %get-tuple-element.73), channel_id=1, source_target_pairs={{0,16},{8,24},{16,0},{24,8},{1,17},{9,25},{17,1},{25,9},{2,18},{10... | collective-permute-start | bytes 393224 | tf_op jit(solution)/shard_map/ppermute | solution.py:220
  47.5 4.8 %collective-permute-start.16 = (bf16[256,256]{1,0:T(8,128)(2,1)S(1)}, bf16[256,256]{1,0:T(8,128)(2,1)S(1)}, u32[]{:S(2)}, u32[]{:S(2)}) collective-permute-start(bf16[256,256]{1,0:T(8,128)(2,1)S(1)} %get-tuple-element.74), channel_id=1, source_target_pairs={{0,8},{8,0},{16,24},{24,16},{1,9},{9,1},{17,25},{25,17},{2,10},{10... | collective-permute-start | bytes 393224 | tf_op jit(solution)/shard_map/ppermute | solution.py:220
  53.2 11.9 %collective-permute-start.21 = (bf16[128,512]{1,0:T(8,128)(2,1)S(1)}, bf16[128,512]{1,0:T(8,128)(2,1)S(1)}, u32[]{:S(2)}, u32[]{:S(2)}) collective-permute-start(bf16[128,512]{1,0:T(8,128)(2,1)S(1)} %get-tuple-element.80), channel_id=1, source_target_pairs={{0,6},{1,7},{2,0},{3,1},{4,2},{5,3},{6,4},{7,5},{8,14},{9,15},{10,... | collective-permute-start | bytes 393224 | tf_op jit(solution)/shard_map/ppermute | solution.py:225
  55.0 13.6 %collective-permute-start.22 = (bf16[128,512]{1,0:T(8,128)(2,1)S(1)}, bf16[128,512]{1,0:T(8,128)(2,1)S(1)}, u32[]{:S(2)}, u32[]{:S(2)}) collective-permute-start(bf16[128,512]{1,0:T(8,128)(2,1)S(1)} %get-tuple-element.81), channel_id=1, source_target_pairs={{0,2},{1,3},{2,4},{3,5},{4,6},{5,7},{6,0},{7,1},{8,10},{9,11},{10,... | collective-permute-start | bytes 393224 | tf_op jit(solution)/shard_map/ppermute | solution.py:225
  59.8 9.0 %collective-permute-start.19 = (bf16[128,512]{1,0:T(8,128)(2,1)S(1)}, bf16[128,512]{1,0:T(8,128)(2,1)S(1)}, u32[]{:S(2)}, u32[]{:S(2)}) collective-permute-start(bf16[128,512]{1,0:T(8,128)(2,1)S(1)} %get-tuple-element.78), channel_id=1, source_target_pairs={{0,7},{1,0},{2,1},{3,2},{4,3},{5,4},{6,5},{7,6},{8,15},{9,8},{10,9... | collective-permute-start | bytes 393224 | tf_op jit(solution)/shard_map/ppermute | solution.py:225
  62.4 6.4 %collective-permute-start.20 = (bf16[128,512]{1,0:T(8,128)(2,1)S(1)}, bf16[128,512]{1,0:T(8,128)(2,1)S(1)}, u32[]{:S(2)}, u32[]{:S(2)}) collective-permute-start(bf16[128,512]{1,0:T(8,128)(2,1)S(1)} %get-tuple-element.79), channel_id=1, source_target_pairs={{0,1},{1,2},{2,3},{3,4},{4,5},{5,6},{6,7},{7,0},{8,9},{9,10},{10,1... | collective-permute-start | bytes 393224 | tf_op jit(solution)/shard_map/ppermute | solution.py:225
  63.0 13.9 %collective-permute-start.17 = (bf16[128,512]{1,0:T(8,128)(2,1)S(1)}, bf16[128,512]{1,0:T(8,128)(2,1)S(1)}, u32[]{:S(2)}, u32[]{:S(2)}) collective-permute-start(bf16[128,512]{1,0:T(8,128)(2,1)S(1)} %get-tuple-element.76), channel_id=1, source_target_pairs={{0,5},{1,6},{2,7},{3,0},{4,1},{5,2},{6,3},{7,4},{8,13},{9,14},{10,... | collective-permute-start | bytes 393224 | tf_op jit(solution)/shard_map/ppermute | solution.py:225
  65.2 11.8 %collective-permute-start.18 = (bf16[128,512]{1,0:T(8,128)(2,1)S(1)}, bf16[128,512]{1,0:T(8,128)(2,1)S(1)}, u32[]{:S(2)}, u32[]{:S(2)}) collective-permute-start(bf16[128,512]{1,0:T(8,128)(2,1)S(1)} %get-tuple-element.77), channel_id=1, source_target_pairs={{0,3},{1,4},{2,5},{3,6},{4,7},{5,0},{6,1},{7,2},{8,11},{9,12},{10,... | collective-permute-start | bytes 393224 | tf_op jit(solution)/shard_map/ppermute | solution.py:225
where the time goes:
time: 79.9 us; the launch traced here: 78.9 us
  starting transfers between devices  35.1 us (44%)
  Pallas kernels  20.4 us (26%)
  waiting for transfers between devices  16.3 us (20%)
  local copies, waits for them, and re-layouts  4.37 us (5%)
  other arithmetic  1.62 us (2%)
  between operations  1.05 us (1%)
    ppermute x12, starting transfers between devices, col_shift(): lax.ppermute(value, 'col', [(s, (s + steps) % count) for s in range(count)])  25.7 us
    pallas_call x20, Pallas kernels, call(): pl.pallas_call(body, out_shape=tuple((jax.ShapeDtypeStruct(o.shape, o.dty...  20.4 us
    ppermute x11, starting transfers between devices, row_move(): return lax.ppermute(value, 'row', [(s, s ^ bit) for s in range(count)])  9.41 us
    ppermute x11, waiting for transfers between devices, row_move(): return lax.ppermute(value, 'row', [(s, s ^ bit) for s in range(count)])  9.15 us
    ppermute x12, waiting for transfers between devices, col_shift(): lax.ppermute(value, 'col', [(s, (s + steps) % count) for s in range(count)])  7.11 us
    unnamed x18, local copies, waits for them, and re-layouts  4.37 us
  transfers between devices with their start and end apart: 23, of which 9 were waited for; matrix products, arithmetic and copies ran while one was open for 2% of the time, Pallas kernels for 18%

commit v1 on v0

--- a/solution.py
+++ b/solution.py
@@ -71,7 +71,8 @@
         at += exact.shape[1]
 
 
-def partial_body(targets_ref, m_ref, *outs):
+def partial_body(targets_ref, m_ref, m_out, *outs):
+    m_out[...] = m_ref[...]
     split_columns(sums_of(targets_ref, 0, m_ref[...], outs[0].shape[0]), outs)
 
 
@@ -105,10 +106,9 @@
 
 
 def pre_body(layer, order_ref, *refs):
-    (w_ref, w_node_ref, out, w_node_out), at = refs[-4:], 0
-    w_node_out[...] = w_node_ref[layer]
+    (w_ref, out), at = refs[-2:], 0
     block = order_ref.shape[1]
-    for ref in refs[:-4]:
+    for ref in refs[:-2]:
         rows = min(ref.shape[0], out.shape[0] - at)
         width = ref.shape[1]
         m_rows = [
@@ -129,8 +129,10 @@
     block, width = outs[0].shape
     table = table_ref[...]
     w = w_ref[layer, width : 2 * width, :]
-    for half, out in enumerate(outs):
-        out[...] = sent_rows(first + half, block, hot_ref, pre_ref, table, w)
+    rows = [pl.ds((first + half) * block, block) for half in range(2)]
+    h_rows = [dot(hot_ref[r, :], table).astype(BF16) for r in rows]
+    for r, h, out in zip(rows, h_rows, outs):
+        out[...] = (pre_ref[r, :] + dot(h, w)).astype(BF16)
 
 
 def edge_blocks(layer, got, m_blocks, w_ref):
@@ -255,7 +257,15 @@
     piece_shapes = [sds(points, piece, t) for piece in pieces for t in (F32, BF16)]
     own = partner_numbers(targets[0], me, share)
     table = [share_h]
-    sums = call(partial_body, piece_shapes, (own, m), 2 * points * edges * width)
+    m, *sums = call(
+        partial_body,
+        [sds(edges, width, BF16)] + piece_shapes,
+        (own, m),
+        2 * points * edges * width,
+    )
+    w_in, w_res, w_node, order, *sums = lax.optimization_barrier(
+        (w_in, w_res, w_node, order, *sums)
+    )
     for k in range(1, count):
         table.append(row_move(share_h, k))
     hot = (own[0][:, None] == jnp.arange(points, dtype=jnp.int32)[None, :]).astype(BF16)
@@ -282,16 +292,16 @@
                 (order, hot),
                 2 * edges * block * points,
             )
-        pre, w_point = call(
+        (pre,) = call(
             functools.partial(pre_body, layer),
-            [sds(edges, width, F32), sds(width, width, BF16)],
-            (order, *((m,) if first else [part for part, _ in m_parts]), w_in, w_node),
+            [sds(edges, width, F32)],
+            (order, *((m,) if first else [part for part, _ in m_parts]), w_in),
             PAIRS * product,
         )
         (h,) = call(
             functools.partial(update_body, bits, share, scale),
             [sds(points, width, BF16)],
-            (w_point, *sums[::2], *got, *table),
+            (w_node[layer], *sums[::2], *got, *table),
             2 * points * width * width,
         )
         table = [h]

time: 79.9 us -> 78.2 us (0.979)
  local copies, waits for them, and re-layouts: 4.37 us -> 2.51 us
  waiting for transfers between devices: 16.3 us -> 17.6 us
  Pallas kernels: 20.4 us -> 19.6 us
    unnamed x18 -> x12, local copies, waits for them, and re-layouts: 4.37 us -> 1.25 us
    squeeze x0 -> x1, local copies, waits for them, and re-layouts: none -> 1.27 us  [shards(): w_node[layer]]
    ppermute x11, waiting for transfers between devices: 9.15 us -> 10.4 us  [row_move(): return lax.ppermute(value, 'row', [(s, s ^ bit) for s in range(count)])]
    pallas_call x20, Pallas kernels: 20.4 us -> 19.6 us  [call(): pl.pallas_call(body, out_shape=tuple((jax.ShapeDtypeStruct(o.shape, o.dty...]
  transfers between devices with their start and end apart: 23 -> 23, of which waited for: 9 -> 11; matrix products, arithmetic and copies ran while one was open for 2% -> 3% of each run, Pallas kernels for 18% -> 18%
where the time goes in v1:
time: 78.2 us; the launch traced here: 77.2 us
  starting transfers between devices  35.5 us (45%)
  Pallas kernels  19.6 us (25%)
  waiting for transfers between devices  17.6 us (23%)
  local copies, waits for them, and re-layouts  2.51 us (3%)
  between operations  1.06 us (1%)
  other arithmetic  0.94 us (1%)
    ppermute x12, starting transfers between devices, col_shift(): lax.ppermute(value, 'col', [(s, (s + steps) % count) for s in range(count)])  26.1 us
    pallas_call x20, Pallas kernels, call(): pl.pallas_call(body, out_shape=tuple((jax.ShapeDtypeStruct(o.shape, o.dty...  19.6 us
    ppermute x11, waiting for transfers between devices, row_move(): return lax.ppermute(value, 'row', [(s, s ^ bit) for s in range(count)])  10.4 us
    ppermute x11, starting transfers between devices, row_move(): return lax.ppermute(value, 'row', [(s, s ^ bit) for s in range(count)])  9.4 us
    ppermute x12, waiting for transfers between devices, col_shift(): lax.ppermute(value, 'col', [(s, (s + steps) % count) for s in range(count)])  7.26 us
  transfers between devices with their start and end apart: 23, of which 11 were waited for; matrix products, arithmetic and copies ran while one was open for 3% of the time, Pallas kernels for 18%

profile of v1, /device:TPU:1, one launch (start us, length us, event | category | flops | bytes accessed | tf_op | source)
XLA Modules:
  0.0 77.2 jit_solution(12553174029018057644)
XLA Ops:
  0.6 3.0 %collective-permute-start.6 = (bf16[64,512]{1,0:T(8,128)(2,1)}, bf16[64,512]{1,0:T(8,128)(2,1)S(1)}, u32[]{:S(2)}, u32[]{:S(2)}) collective-permute-start(bf16[64,512]{1,0:T(8,128)(2,1)} %bitcast.24), channel_id=1, source_target_pairs={{0,24},{8,16},{16,8},{24,0},{1,25},{9,17},{17,9},{25,1},{2,26},{10... | collective-permute-start | bytes 196616 | tf_op jit(solution)/shard_map/ppermute | solution.py:222
  3.7 0.2 collective-permute-start.5
  3.9 0.1 collective-permute-start.4
  4.1 0.7 fusion.1.targets_ref.refs_0_
  4.8 0.0 copy-start.2
  4.8 1.2 %copy-done.2 = bf16[1,1,1024,512]{3,2,1,0:T(8,128)(2,1)S(1)} copy-done((bf16[1,1,1024,512]{3,2,1,0:T(8,128)(2,1)S(1)}, bf16[1,1,1024,512]{3,2,1,0:T(8,128)(2,1)}, u32[]{:S(2)}) %copy-start.2) | copy-done | bytes 1048600
  6.0 0.5 shard_map.86
  6.5 0.0 copy-start
  6.5 1.4 %collective-permute-start = (bf16[256,256]{1,0:T(8,128)(2,1)S(1)}, bf16[256,256]{1,0:T(8,128)(2,1)S(1)}, u32[]{:S(2)}, u32[]{:S(2)}) collective-permute-start(bf16[256,256]{1,0:T(8,128)(2,1)S(1)} %get-tuple-element.58), channel_id=1, source_target_pairs={{0,8},{8,0},{16,24},{24,16},{1,9},{9,1},{17,25},{25,17},{2,10},{10... | collective-permute-start | bytes 393224 | tf_op jit(solution)/shard_map/ppermute | solution.py:222
  7.9 1.2 %collective-permute-start.1 = (bf16[256,256]{1,0:T(8,128)(2,1)S(1)}, bf16[256,256]{1,0:T(8,128)(2,1)S(1)}, u32[]{:S(2)}, u32[]{:S(2)}) collective-permute-start(bf16[256,256]{1,0:T(8,128)(2,1)S(1)} %get-tuple-element.59), channel_id=1, source_target_pairs={{0,16},{8,24},{16,0},{24,8},{1,17},{9,25},{17,1},{25,9},{2,18},{10... | collective-permute-start | bytes 393224 | tf_op jit(solution)/shard_map/ppermute | solution.py:222
  9.2 1.3 %slice_bitcast_fusion = (bf16[512,512]{1,0:T(8,128)(2,1)S(1)}, bf16[512,512]{1,0:T(8,128)(2,1)S(1)}) fusion(bf16[2,512,512]{2,1,0:T(8,128)(2,1)} %param.13), kind=kLoop, calls=%fused_computation.2 | loop fusion | bytes 2097152 | tf_op jit(solution)/shard_map/squeeze | solution.py:304
  10.5 0.0 collective-permute-done.refs_2_
  10.5 1.6 %collective-permute-done.1.refs_3_ = bf16[256,256]{1,0:T(8,128)(2,1)S(1)} collective-permute-done((bf16[256,256]{1,0:T(8,128)(2,1)S(1)}, bf16[256,256]{1,0:T(8,128)(2,1)S(1)}, u32[]{:S(2)}, u32[]{:S(2)}) %collective-permute-start.1) | collective-permute-done | bytes 131104 | tf_op jit(solution)/shard_map/ppermute | solution.py:222
  12.0 0.1 shard_map.89
  12.1 1.3 %collective-permute-start.2 = (bf16[256,256]{1,0:T(8,128)(2,1)S(1)}, bf16[256,256]{1,0:T(8,128)(2,1)S(1)}, u32[]{:S(2)}, u32[]{:S(2)}) collective-permute-start(bf16[256,256]{1,0:T(8,128)(2,1)S(1)} %get-tuple-element.62), channel_id=1, source_target_pairs={{0,16},{8,24},{16,0},{24,8},{1,17},{9,25},{17,1},{25,9},{2,18},{10... | collective-permute-start | bytes 393224 | tf_op jit(solution)/shard_map/ppermute | solution.py:222
  13.4 0.2 fusion.hot_ref
  13.6 0.3 shard_map.87.sent_ref.hot_ref
  13.9 0.0 copy-start.3
  13.9 1.0 %shard_map.88.pre_ref = f32[1024,512]{1,0:T(8,128)S(1)} custom-call(s32[8,128]{1,0:T(8,128)S(1)} %bitcast.29, bf16[1024,512]{1,0:T(8,128)(2,1)S(1)} %get-tuple-element.53.refs_0_.m_ref, bf16[2,1536,512]{2,1,0:T(8,128)(2,1)S(1)} %copy-done), custom_call_target="tpu_custom_call" | custom-call | flops 536870912 | bytes 6295552 | tf_op jit(solution)/shard_map/pallas_call | solution.py:30
  14.9 0.0 collective-permute-done.5.refs_6_
  14.9 0.0 collective-permute-done.4.refs_5_
  14.9 1.0 %collective-permute-done.2.refs_2_ = bf16[256,256]{1,0:T(8,128)(2,1)S(1)} collective-permute-done((bf16[256,256]{1,0:T(8,128)(2,1)S(1)}, bf16[256,256]{1,0:T(8,128)(2,1)S(1)}, u32[]{:S(2)}, u32[]{:S(2)}) %collective-permute-start.2) | collective-permute-done | bytes 131104 | tf_op jit(solution)/shard_map/ppermute | solution.py:222
  16.0 1.2 %collective-permute-done.3.refs_3_ = bf16[256,256]{1,0:T(8,128)(2,1)S(1)} collective-permute-done((bf16[256,256]{1,0:T(8,128)(2,1)S(1)}, bf16[256,256]{1,0:T(8,128)(2,1)S(1)}, u32[]{:S(2)}, u32[]{:S(2)}) %collective-permute-start.3) | collective-permute-done | bytes 131104 | tf_op jit(solution)/shard_map/ppermute | solution.py:222
  17.2 0.4 shard_map.90.table_ref.refs_4_
  17.6 0.4 shard_map.95
  18.1 0.4 shard_map.93
  18.5 0.0 copy-start.1
  18.5 0.4 shard_map.92
  19.0 7.3 %collective-permute-start.11 = (bf16[128,512]{1,0:T(8,128)(2,1)S(1)}, bf16[128,512]{1,0:T(8,128)(2,1)S(1)}, u32[]{:S(2)}, u32[]{:S(2)}) collective-permute-start(bf16[128,512]{1,0:T(8,128)(2,1)S(1)} %get-tuple-element.74), channel_id=1, source_target_pairs={{0,5},{1,6},{2,7},{3,0},{4,1},{5,2},{6,3},{7,4},{8,13},{9,14},{10,... | collective-permute-start | bytes 393224 | tf_op jit(solution)/shard_map/ppermute | solution.py:227
  26.3 0.2 collective-permute-start.9
  26.5 1.3 %collective-permute-start.10 = (bf16[128,512]{1,0:T(8,128)(2,1)S(1)}, bf16[128,512]{1,0:T(8,128)(2,1)S(1)}, u32[]{:S(2)}, u32[]{:S(2)}) collective-permute-start(bf16[128,512]{1,0:T(8,128)(2,1)S(1)} %get-tuple-element.71), channel_id=1, source_target_pairs={{0,2},{1,3},{2,4},{3,5},{4,6},{5,7},{6,0},{7,1},{8,10},{9,11},{10,... | collective-permute-start | bytes 393224 | tf_op jit(solution)/shard_map/ppermute | solution.py:227
  27.8 0.0 collective-permute-start.7
  27.8 1.7 %collective-permute-start.8 = (bf16[128,512]{1,0:T(8,128)(2,1)S(1)}, bf16[128,512]{1,0:T(8,128)(2,1)S(1)}, u32[]{:S(2)}, u32[]{:S(2)}) collective-permute-start(bf16[128,512]{1,0:T(8,128)(2,1)S(1)} %get-tuple-element.69), channel_id=1, source_target_pairs={{0,1},{1,2},{2,3},{3,4},{4,5},{5,6},{6,7},{7,0},{8,9},{9,10},{10,1... | collective-permute-start | bytes 393224 | tf_op jit(solution)/shard_map/ppermute | solution.py:227
  29.5 2.4 %shard_map.91 = (f32[768,512]{1,0:T(8,128)S(1)}, bf16[256,512]{1,0:T(8,128)(2,1)S(1)}, f32[256,512]{1,0:T(8,128)S(1)}) custom-call(bf16[1024,256]{1,0:T(8,128)(2,1)S(1)} %fusion.hot_ref, bf16[1024,256]{1,0:T(8,128)(2,1)S(1)} %shard_map.87.sent_ref.hot_ref, f32[1024,512]{1,0:T(8,128)S(1)} %shard_map.88.pre_ref, ...), custom_call_target="tpu_custom_call" | custom-call | flops 1610612736 | bytes 14159872 | tf_op jit(solution)/shard_map/pallas_call | solution.py:30
  31.9 4.5 %collective-permute-start.12 = (bf16[128,512]{1,0:T(8,128)(2,1)S(1)}, bf16[128,512]{1,0:T(8,128)(2,1)S(1)}, u32[]{:S(2)}, u32[]{:S(2)}) collective-permute-start(bf16[128,512]{1,0:T(8,128)(2,1)S(1)} %get-tuple-element.75), channel_id=1, source_target_pairs={{0,3},{1,4},{2,5},{3,6},{4,7},{5,0},{6,1},{7,2},{8,11},{9,12},{10,... | collective-permute-start | bytes 393224 | tf_op jit(solution)/shard_map/ppermute | solution.py:227
  36.4 0.0 collective-permute-done.10.refs_3_
  36.4 0.3 collective-permute-done.8.refs_1_
  36.7 2.2 %shard_map.94 = (bf16[512,512]{1,0:T(8,128)(2,1)S(1)}, f32[256,512]{1,0:T(8,128)S(1)}) custom-call(f32[768,512]{1,0:T(8,128)S(1)} %get-tuple-element.66.part_ref, bf16[1024,512]{1,0:T(8,128)(2,1)S(1)} %get-tuple-element.53.refs_0_.m_ref, bf16[2,2,2,512,512]{4,3,2,1,0:T(8,128)(2,1)S(1)} %copy-done.1, s32[1,1024]{1,0:T(1,128)S(1)} %fusion.1.targets_ref.refs_0_, ...), custom_call_target="tpu_custom_call" | custom-call | flops 1610612736 | bytes 8916992 | tf_op jit(solution)/shard_map/pallas_call | solution.py:30
  38.9 1.2 %collective-permute-done.12.refs_1_ = bf16[128,512]{1,0:T(8,128)(2,1)S(1)} collective-permute-done((bf16[128,512]{1,0:T(8,128)(2,1)S(1)}, bf16[128,512]{1,0:T(8,128)(2,1)S(1)}, u32[]{:S(2)}, u32[]{:S(2)}) %collective-permute-start.12) | collective-permute-done | bytes 131104 | tf_op jit(solution)/shard_map/ppermute | solution.py:227
  40.1 1.3 %shard_map.96 = (bf16[256,512]{1,0:T(8,128)(2,1)S(1)}, f32[256,256]{1,0:T(8,128)S(1)}, bf16[256,256]{1,0:T(8,128)(2,1)S(1)}, f32[256,256]{1,0:T(8,128)S(1)}, bf16[256,256]{1,0:T(8,128)(2,1)S(1)}) custom-call(f32[768,512]{1,0:T(8,128)S(1)} %get-tuple-element.66.part_ref, bf16[1024,512]{1,0:T(8,128)(2,1)S(1)} %get-tuple-element.53.refs_0_.m_ref, ...), custom_call_target="tpu_custom_call" | custom-call | flops 805306368 | bytes 8654848 | tf_op jit(solution)/shard_map/pallas_call | solution.py:30
  41.4 0.3 collective-permute-start.13
  41.8 0.2 collective-permute-start.14
  42.0 3.3 %collective-permute-done.13.refs_2_ = bf16[256,256]{1,0:T(8,128)(2,1)S(1)} collective-permute-done((bf16[256,256]{1,0:T(8,128)(2,1)S(1)}, bf16[256,256]{1,0:T(8,128)(2,1)S(1)}, u32[]{:S(2)}, u32[]{:S(2)}) %collective-permute-start.13) | collective-permute-done | bytes 131104 | tf_op jit(solution)/shard_map/ppermute | solution.py:222
  45.3 0.3 collective-permute-done.14.refs_3_
  45.6 0.1 shard_map.98
  45.7 0.3 collective-permute-start.15
  46.0 1.2 %collective-permute-start.16 = (bf16[256,256]{1,0:T(8,128)(2,1)S(1)}, bf16[256,256]{1,0:T(8,128)(2,1)S(1)}, u32[]{:S(2)}, u32[]{:S(2)}) collective-permute-start(bf16[256,256]{1,0:T(8,128)(2,1)S(1)} %get-tuple-element.84), channel_id=1, source_target_pairs={{0,8},{8,0},{16,24},{24,16},{1,9},{9,1},{17,25},{25,17},{2,10},{10... | collective-permute-start | bytes 393224 | tf_op jit(solution)/shard_map/ppermute | solution.py:222
  47.2 1.1 %shard_map.97.pre_ref = f32[1024,512]{1,0:T(8,128)S(1)} custom-call(s32[8,128]{1,0:T(8,128)S(1)} %bitcast.30, bf16[256,512]{1,0:T(8,128)(2,1)S(1)} %get-tuple-element.65.refs_0_.m_ref, bf16[512,512]{1,0:T(8,128)(2,1)S(1)} %get-tuple-element.72.refs_1_.m_ref, bf16[256,512]{1,0:T(8,128)(2,1)S(1)} %get-tuple-element.76.refs_2_.m_ref, ...), custom_call_target="tpu_custom_call" | custom-call | flops 536870912 | bytes 6295552 | tf_op jit(solution)/shard_map/pallas_call | solution.py:30
  48.3 2.5 %collective-permute-done.15.refs_2_ = bf16[256,256]{1,0:T(8,128)(2,1)S(1)} collective-permute-done((bf16[256,256]{1,0:T(8,128)(2,1)S(1)}, bf16[256,256]{1,0:T(8,128)(2,1)S(1)}, u32[]{:S(2)}, u32[]{:S(2)}) %collective-permute-start.15) | collective-permute-done | bytes 131104 | tf_op jit(solution)/shard_map/ppermute | solution.py:222
  50.8 0.4 collective-permute-done.16.refs_3_
  51.2 0.4 shard_map.99.table_ref
  51.6 0.4 shard_map.103
  52.0 1.0 %collective-permute-start.21 = (bf16[128,512]{1,0:T(8,128)(2,1)S(1)}, bf16[128,512]{1,0:T(8,128)(2,1)S(1)}, u32[]{:S(2)}, u32[]{:S(2)}) collective-permute-start(bf16[128,512]{1,0:T(8,128)(2,1)S(1)} %get-tuple-element.90), channel_id=1, source_target_pairs={{0,6},{1,7},{2,0},{3,1},{4,2},{5,3},{6,4},{7,5},{8,14},{9,15},{10,... | collective-permute-start | bytes 393224 | tf_op jit(solution)/shard_map/ppermute | solution.py:227
  53.1 4.4 %collective-permute-start.22 = (bf16[128,512]{1,0:T(8,128)(2,1)S(1)}, bf16[128,512]{1,0:T(8,128)(2,1)S(1)}, u32[]{:S(2)}, u32[]{:S(2)}) collective-permute-start(bf16[128,512]{1,0:T(8,128)(2,1)S(1)} %get-tuple-element.91), channel_id=1, source_target_pairs={{0,2},{1,3},{2,4},{3,5},{4,6},{5,7},{6,0},{7,1},{8,10},{9,11},{10,... | collective-permute-start | bytes 393224 | tf_op jit(solution)/shard_map/ppermute | solution.py:227
  57.5 0.4 shard_map.102
  58.0 2.7 %collective-permute-start.19 = (bf16[128,512]{1,0:T(8,128)(2,1)S(1)}, bf16[128,512]{1,0:T(8,128)(2,1)S(1)}, u32[]{:S(2)}, u32[]{:S(2)}) collective-permute-start(bf16[128,512]{1,0:T(8,128)(2,1)S(1)} %get-tuple-element.88), channel_id=1, source_target_pairs={{0,7},{1,0},{2,1},{3,2},{4,3},{5,4},{6,5},{7,6},{8,15},{9,8},{10,9... | collective-permute-start | bytes 393224 | tf_op jit(solution)/shard_map/ppermute | solution.py:227
  60.7 0.4 shard_map.101
  61.1 2.0 %collective-permute-start.17 = (bf16[128,512]{1,0:T(8,128)(2,1)S(1)}, bf16[128,512]{1,0:T(8,128)(2,1)S(1)}, u32[]{:S(2)}, u32[]{:S(2)}) collective-permute-start(bf16[128,512]{1,0:T(8,128)(2,1)S(1)} %get-tuple-element.86), channel_id=1, source_target_pairs={{0,5},{1,6},{2,7},{3,0},{4,1},{5,2},{6,3},{7,4},{8,13},{9,14},{10,... | collective-permute-start | bytes 393224 | tf_op jit(solution)/shard_map/ppermute | solution.py:227
  63.1 0.8 %collective-permute-start.18 = (bf16[128,512]{1,0:T(8,128)(2,1)S(1)}, bf16[128,512]{1,0:T(8,128)(2,1)S(1)}, u32[]{:S(2)}, u32[]{:S(2)}) collective-permute-start(bf16[128,512]{1,0:T(8,128)(2,1)S(1)} %get-tuple-element.87), channel_id=1, source_target_pairs={{0,3},{1,4},{2,5},{3,6},{4,7},{5,0},{6,1},{7,2},{8,11},{9,12},{10,... | collective-permute-start | bytes 393224 | tf_op jit(solution)/shard_map/ppermute | solution.py:227
  64.0 2.9 %shard_map.100 = (f32[768,512]{1,0:T(8,128)S(1)}, bf16[256,512]{1,0:T(8,128)(2,1)S(1)}, bf16[64,512]{1,0:T(8,128)(2,1)}) custom-call(bf16[1024,256]{1,0:T(8,128)(2,1)S(1)} %fusion.hot_ref, bf16[1024,256]{1,0:T(8,128)(2,1)S(1)} %shard_map.87.sent_ref.hot_ref, f32[1024,512]{1,0:T(8,128)S(1)} %shard_map.97.pre_ref, bf16[256,512]{1,0:T(8,128)(2,1)S(1)} %shard_map.99.table_ref, ...), custom_call_target="tpu_custom_call" | custom-call | flops 1610612736 | bytes 12910592 | tf_op jit(solution)/shard_map/pallas_call | solution.py:30
  66.9 0.3 collective-permute-done.19.refs_0_
  67.1 2.6 %shard_map.104.refs_2_ = bf16[1024,512]{1,0:T(8,128)(2,1)} custom-call(f32[768,512]{1,0:T(8,128)S(1)} %get-tuple-element.85.part_ref, bf16[512,512]{1,0:T(8,128)(2,1)S(1)} %get-tuple-element.72.refs_1_.m_ref, bf16[2,2,2,512,512]{4,3,2,1,0:T(8,128)(2,1)S(1)} %copy-done.1, bf16[128,512]{1,0:T(8,128)(2,1)S(1)} %collective-permute-done.19.refs_0_, ...), custom_call_target="tpu_custom_call" | custom-call | flops 1073741824 | bytes 8126464 | tf_op jit(solution)/shard_map/pallas_call | solution.py:30
  69.8 5.5 %collective-permute-done.17.refs_0_ = bf16[128,512]{1,0:T(8,128)(2,1)S(1)} collective-permute-done((bf16[128,512]{1,0:T(8,128)(2,1)S(1)}, bf16[128,512]{1,0:T(8,128)(2,1)S(1)}, u32[]{:S(2)}, u32[]{:S(2)}) %collective-permute-start.17) | collective-permute-done | bytes 131104 | tf_op jit(solution)/shard_map/ppermute | solution.py:227
  75.3 1.8 %shard_map.105 = bf16[1024,512]{1,0:T(8,128)(2,1)} custom-call(f32[768,512]{1,0:T(8,128)S(1)} %get-tuple-element.85.part_ref, bf16[256,512]{1,0:T(8,128)(2,1)S(1)} %get-tuple-element.76.refs_2_.m_ref, bf16[2,2,2,512,512]{4,3,2,1,0:T(8,128)(2,1)S(1)} %copy-done.1, ...), custom_call_target="tpu_custom_call", output_to_operand_aliasing={{}: (5, {})} | custom-call | flops 536870912 | bytes 8388608 | tf_op jit(solution)/shard_map/pallas_call | solution.py:30
  (18 shorter events, 0.1 us)
Async XLA Ops:
  0.6 9.8 %copy-start.5 = (s32[1,1,1024]{2,1,0:T(1,128)S(1)}, s32[1,1,1024]{2,1,0:T(1,128)}, u32[]{:S(2)}) copy-start(s32[1,1,1024]{2,1,0:T(1,128)} %param.8) | copy-start | bytes 12292
  0.6 14.3 %collective-permute-start.6 = (bf16[64,512]{1,0:T(8,128)(2,1)}, bf16[64,512]{1,0:T(8,128)(2,1)S(1)}, u32[]{:S(2)}, u32[]{:S(2)}) collective-permute-start(bf16[64,512]{1,0:T(8,128)(2,1)} %bitcast.24), channel_id=1, source_target_pairs={{0,24},{8,16},{16,8},{24,0},{1,25},{9,17},{17,9},{25,1},{2,26},{10... | collective-permute-start | bytes 196616 | tf_op jit(solution)/shard_map/ppermute | solution.py:222
  3.7 11.2 %collective-permute-start.5 = (bf16[64,512]{1,0:T(8,128)(2,1)}, bf16[64,512]{1,0:T(8,128)(2,1)S(1)}, u32[]{:S(2)}, u32[]{:S(2)}) collective-permute-start(bf16[64,512]{1,0:T(8,128)(2,1)} %bitcast.25), channel_id=1, source_target_pairs={{0,16},{8,24},{16,0},{24,8},{1,17},{9,25},{17,1},{25,9},{2,18},{10... | collective-permute-start | bytes 196616 | tf_op jit(solution)/shard_map/ppermute | solution.py:222
  3.9 11.0 %collective-permute-start.4 = (bf16[64,512]{1,0:T(8,128)(2,1)}, bf16[64,512]{1,0:T(8,128)(2,1)S(1)}, u32[]{:S(2)}, u32[]{:S(2)}) collective-permute-start(bf16[64,512]{1,0:T(8,128)(2,1)} %bitcast.26), channel_id=1, source_target_pairs={{0,8},{8,0},{16,24},{24,16},{1,9},{9,1},{17,25},{25,17},{2,10},{10... | collective-permute-start | bytes 196616 | tf_op jit(solution)/shard_map/ppermute | solution.py:222
  4.8 1.2 %copy-start.2 = (bf16[1,1,1024,512]{3,2,1,0:T(8,128)(2,1)S(1)}, bf16[1,1,1024,512]{3,2,1,0:T(8,128)(2,1)}, u32[]{:S(2)}) copy-start(bf16[1,1,1024,512]{3,2,1,0:T(8,128)(2,1)} %param.7) | copy-start | bytes 3145732
  6.0 7.6 %copy-start.4 = (s32[1,1,8,128]{3,2,1,0:T(8,128)S(1)}, s32[1,1,8,128]{3,2,1,0:T(8,128)}, u32[]{:S(2)}) copy-start(s32[1,1,8,128]{3,2,1,0:T(8,128)} %param.9) | copy-start | bytes 12292
  6.5 7.4 %copy-start = (bf16[2,1536,512]{2,1,0:T(8,128)(2,1)S(1)}, bf16[2,1536,512]{2,1,0:T(8,128)(2,1)}, u32[]{:S(2)}) copy-start(bf16[2,1536,512]{2,1,0:T(8,128)(2,1)} %w_ref.9) | copy-start | bytes 9437188
  6.5 3.9 %collective-permute-start = (bf16[256,256]{1,0:T(8,128)(2,1)S(1)}, bf16[256,256]{1,0:T(8,128)(2,1)S(1)}, u32[]{:S(2)}, u32[]{:S(2)}) collective-permute-start(bf16[256,256]{1,0:T(8,128)(2,1)S(1)} %get-tuple-element.58), channel_id=1, source_target_pairs={{0,8},{8,0},{16,24},{24,16},{1,9},{9,1},{17,25},{25,17},{2,10},{10... | collective-permute-start | bytes 393224 | tf_op jit(solution)/shard_map/ppermute | solution.py:222
  7.9 4.1 %collective-permute-start.1 = (bf16[256,256]{1,0:T(8,128)(2,1)S(1)}, bf16[256,256]{1,0:T(8,128)(2,1)S(1)}, u32[]{:S(2)}, u32[]{:S(2)}) collective-permute-start(bf16[256,256]{1,0:T(8,128)(2,1)S(1)} %get-tuple-element.59), channel_id=1, source_target_pairs={{0,16},{8,24},{16,0},{24,8},{1,17},{9,25},{17,1},{25,9},{2,18},{10... | collective-permute-start | bytes 393224 | tf_op jit(solution)/shard_map/ppermute | solution.py:222
  12.1 3.9 %collective-permute-start.2 = (bf16[256,256]{1,0:T(8,128)(2,1)S(1)}, bf16[256,256]{1,0:T(8,128)(2,1)S(1)}, u32[]{:S(2)}, u32[]{:S(2)}) collective-permute-start(bf16[256,256]{1,0:T(8,128)(2,1)S(1)} %get-tuple-element.62), channel_id=1, source_target_pairs={{0,16},{8,24},{16,0},{24,8},{1,17},{9,25},{17,1},{25,9},{2,18},{10... | collective-permute-start | bytes 393224 | tf_op jit(solution)/shard_map/ppermute | solution.py:222
  13.4 3.8 %collective-permute-start.3 = (bf16[256,256]{1,0:T(8,128)(2,1)S(1)}, bf16[256,256]{1,0:T(8,128)(2,1)S(1)}, u32[]{:S(2)}, u32[]{:S(2)}) collective-permute-start(bf16[256,256]{1,0:T(8,128)(2,1)S(1)} %get-tuple-element.63), channel_id=1, source_target_pairs={{0,8},{8,0},{16,24},{24,16},{1,9},{9,1},{17,25},{25,17},{2,10},{10... | collective-permute-start | bytes 393224 | tf_op jit(solution)/shard_map/ppermute | solution.py:222
  13.9 3.3 %copy-start.3 = (bf16[1,64,512]{2,1,0:T(8,128)(2,1)S(1)}, bf16[1,64,512]{2,1,0:T(8,128)(2,1)}, u32[]{:S(2)}) copy-start(bf16[1,64,512]{2,1,0:T(8,128)(2,1)} %param.10) | copy-start | bytes 196612
  18.5 11.0 %copy-start.1 = (bf16[2,2,2,512,512]{4,3,2,1,0:T(8,128)(2,1)S(1)}, bf16[2,2,2,512,512]{4,3,2,1,0:T(8,128)(2,1)}, u32[]{:S(2)}) copy-start(bf16[2,2,2,512,512]{4,3,2,1,0:T(8,128)(2,1)} %w_ref.11) | copy-start | bytes 12582916
  19.0 19.9 %collective-permute-start.11 = (bf16[128,512]{1,0:T(8,128)(2,1)S(1)}, bf16[128,512]{1,0:T(8,128)(2,1)S(1)}, u32[]{:S(2)}, u32[]{:S(2)}) collective-permute-start(bf16[128,512]{1,0:T(8,128)(2,1)S(1)} %get-tuple-element.74), channel_id=1, source_target_pairs={{0,5},{1,6},{2,7},{3,0},{4,1},{5,2},{6,3},{7,4},{8,13},{9,14},{10,... | collective-permute-start | bytes 393224 | tf_op jit(solution)/shard_map/ppermute | solution.py:227
  26.3 5.6 %collective-permute-start.9 = (bf16[128,512]{1,0:T(8,128)(2,1)S(1)}, bf16[128,512]{1,0:T(8,128)(2,1)S(1)}, u32[]{:S(2)}, u32[]{:S(2)}) collective-permute-start(bf16[128,512]{1,0:T(8,128)(2,1)S(1)} %get-tuple-element.70), channel_id=1, source_target_pairs={{0,6},{1,7},{2,0},{3,1},{4,2},{5,3},{6,4},{7,5},{8,14},{9,15},{10,... | collective-permute-start | bytes 393224 | tf_op jit(solution)/shard_map/ppermute | solution.py:227
  26.5 9.9 %collective-permute-start.10 = (bf16[128,512]{1,0:T(8,128)(2,1)S(1)}, bf16[128,512]{1,0:T(8,128)(2,1)S(1)}, u32[]{:S(2)}, u32[]{:S(2)}) collective-permute-start(bf16[128,512]{1,0:T(8,128)(2,1)S(1)} %get-tuple-element.71), channel_id=1, source_target_pairs={{0,2},{1,3},{2,4},{3,5},{4,6},{5,7},{6,0},{7,1},{8,10},{9,11},{10,... | collective-permute-start | bytes 393224 | tf_op jit(solution)/shard_map/ppermute | solution.py:227
  27.8 8.6 %collective-permute-start.7 = (bf16[128,512]{1,0:T(8,128)(2,1)S(1)}, bf16[128,512]{1,0:T(8,128)(2,1)S(1)}, u32[]{:S(2)}, u32[]{:S(2)}) collective-permute-start(bf16[128,512]{1,0:T(8,128)(2,1)S(1)} %get-tuple-element.68), channel_id=1, source_target_pairs={{0,7},{1,0},{2,1},{3,2},{4,3},{5,4},{6,5},{7,6},{8,15},{9,8},{10,9... | collective-permute-start | bytes 393224 | tf_op jit(solution)/shard_map/ppermute | solution.py:227
  27.8 8.9 %collective-permute-start.8 = (bf16[128,512]{1,0:T(8,128)(2,1)S(1)}, bf16[128,512]{1,0:T(8,128)(2,1)S(1)}, u32[]{:S(2)}, u32[]{:S(2)}) collective-permute-start(bf16[128,512]{1,0:T(8,128)(2,1)S(1)} %get-tuple-element.69), channel_id=1, source_target_pairs={{0,1},{1,2},{2,3},{3,4},{4,5},{5,6},{6,7},{7,0},{8,9},{9,10},{10,1... | collective-permute-start | bytes 393224 | tf_op jit(solution)/shard_map/ppermute | solution.py:227
  31.9 8.2 %collective-permute-start.12 = (bf16[128,512]{1,0:T(8,128)(2,1)S(1)}, bf16[128,512]{1,0:T(8,128)(2,1)S(1)}, u32[]{:S(2)}, u32[]{:S(2)}) collective-permute-start(bf16[128,512]{1,0:T(8,128)(2,1)S(1)} %get-tuple-element.75), channel_id=1, source_target_pairs={{0,3},{1,4},{2,5},{3,6},{4,7},{5,0},{6,1},{7,2},{8,11},{9,12},{10,... | collective-permute-start | bytes 393224 | tf_op jit(solution)/shard_map/ppermute | solution.py:227
  41.4 3.9 %collective-permute-start.13 = (bf16[256,256]{1,0:T(8,128)(2,1)S(1)}, bf16[256,256]{1,0:T(8,128)(2,1)S(1)}, u32[]{:S(2)}, u32[]{:S(2)}) collective-permute-start(bf16[256,256]{1,0:T(8,128)(2,1)S(1)} %get-tuple-element.79), channel_id=1, source_target_pairs={{0,8},{8,0},{16,24},{24,16},{1,9},{9,1},{17,25},{25,17},{2,10},{10... | collective-permute-start | bytes 393224 | tf_op jit(solution)/shard_map/ppermute | solution.py:222
  41.8 3.8 %collective-permute-start.14 = (bf16[256,256]{1,0:T(8,128)(2,1)S(1)}, bf16[256,256]{1,0:T(8,128)(2,1)S(1)}, u32[]{:S(2)}, u32[]{:S(2)}) collective-permute-start(bf16[256,256]{1,0:T(8,128)(2,1)S(1)} %get-tuple-element.80), channel_id=1, source_target_pairs={{0,16},{8,24},{16,0},{24,8},{1,17},{9,25},{17,1},{25,9},{2,18},{10... | collective-permute-start | bytes 393224 | tf_op jit(solution)/shard_map/ppermute | solution.py:222
  45.7 5.1 %collective-permute-start.15 = (bf16[256,256]{1,0:T(8,128)(2,1)S(1)}, bf16[256,256]{1,0:T(8,128)(2,1)S(1)}, u32[]{:S(2)}, u32[]{:S(2)}) collective-permute-start(bf16[256,256]{1,0:T(8,128)(2,1)S(1)} %get-tuple-element.83), channel_id=1, source_target_pairs={{0,16},{8,24},{16,0},{24,8},{1,17},{9,25},{17,1},{25,9},{2,18},{10... | collective-permute-start | bytes 393224 | tf_op jit(solution)/shard_map/ppermute | solution.py:222
  46.0 5.2 %collective-permute-start.16 = (bf16[256,256]{1,0:T(8,128)(2,1)S(1)}, bf16[256,256]{1,0:T(8,128)(2,1)S(1)}, u32[]{:S(2)}, u32[]{:S(2)}) collective-permute-start(bf16[256,256]{1,0:T(8,128)(2,1)S(1)} %get-tuple-element.84), channel_id=1, source_target_pairs={{0,8},{8,0},{16,24},{24,16},{1,9},{9,1},{17,25},{25,17},{2,10},{10... | collective-permute-start | bytes 393224 | tf_op jit(solution)/shard_map/ppermute | solution.py:222
  52.0 11.1 %collective-permute-start.21 = (bf16[128,512]{1,0:T(8,128)(2,1)S(1)}, bf16[128,512]{1,0:T(8,128)(2,1)S(1)}, u32[]{:S(2)}, u32[]{:S(2)}) collective-permute-start(bf16[128,512]{1,0:T(8,128)(2,1)S(1)} %get-tuple-element.90), channel_id=1, source_target_pairs={{0,6},{1,7},{2,0},{3,1},{4,2},{5,3},{6,4},{7,5},{8,14},{9,15},{10,... | collective-permute-start | bytes 393224 | tf_op jit(solution)/shard_map/ppermute | solution.py:227
  53.1 13.8 %collective-permute-start.22 = (bf16[128,512]{1,0:T(8,128)(2,1)S(1)}, bf16[128,512]{1,0:T(8,128)(2,1)S(1)}, u32[]{:S(2)}, u32[]{:S(2)}) collective-permute-start(bf16[128,512]{1,0:T(8,128)(2,1)S(1)} %get-tuple-element.91), channel_id=1, source_target_pairs={{0,2},{1,3},{2,4},{3,5},{4,6},{5,7},{6,0},{7,1},{8,10},{9,11},{10,... | collective-permute-start | bytes 393224 | tf_op jit(solution)/shard_map/ppermute | solution.py:227
  58.0 9.2 %collective-permute-start.19 = (bf16[128,512]{1,0:T(8,128)(2,1)S(1)}, bf16[128,512]{1,0:T(8,128)(2,1)S(1)}, u32[]{:S(2)}, u32[]{:S(2)}) collective-permute-start(bf16[128,512]{1,0:T(8,128)(2,1)S(1)} %get-tuple-element.88), channel_id=1, source_target_pairs={{0,7},{1,0},{2,1},{3,2},{4,3},{5,4},{6,5},{7,6},{8,15},{9,8},{10,9... | collective-permute-start | bytes 393224 | tf_op jit(solution)/shard_map/ppermute | solution.py:227
  60.7 6.5 %collective-permute-start.20 = (bf16[128,512]{1,0:T(8,128)(2,1)S(1)}, bf16[128,512]{1,0:T(8,128)(2,1)S(1)}, u32[]{:S(2)}, u32[]{:S(2)}) collective-permute-start(bf16[128,512]{1,0:T(8,128)(2,1)S(1)} %get-tuple-element.89), channel_id=1, source_target_pairs={{0,1},{1,2},{2,3},{3,4},{4,5},{5,6},{6,7},{7,0},{8,9},{9,10},{10,1... | collective-permute-start | bytes 393224 | tf_op jit(solution)/shard_map/ppermute | solution.py:227
  61.1 14.2 %collective-permute-start.17 = (bf16[128,512]{1,0:T(8,128)(2,1)S(1)}, bf16[128,512]{1,0:T(8,128)(2,1)S(1)}, u32[]{:S(2)}, u32[]{:S(2)}) collective-permute-start(bf16[128,512]{1,0:T(8,128)(2,1)S(1)} %get-tuple-element.86), channel_id=1, source_target_pairs={{0,5},{1,6},{2,7},{3,0},{4,1},{5,2},{6,3},{7,4},{8,13},{9,14},{10,... | collective-permute-start | bytes 393224 | tf_op jit(solution)/shard_map/ppermute | solution.py:227
  63.1 12.1 %collective-permute-start.18 = (bf16[128,512]{1,0:T(8,128)(2,1)S(1)}, bf16[128,512]{1,0:T(8,128)(2,1)S(1)}, u32[]{:S(2)}, u32[]{:S(2)}) collective-permute-start(bf16[128,512]{1,0:T(8,128)(2,1)S(1)} %get-tuple-element.87), channel_id=1, source_target_pairs={{0,3},{1,4},{2,5},{3,6},{4,7},{5,0},{6,1},{7,2},{8,11},{9,12},{10,... | collective-permute-start | bytes 393224 | tf_op jit(solution)/shard_map/ppermute | solution.py:227

commit v2 on v1

--- a/solution.py
+++ b/solution.py
@@ -90,12 +90,14 @@
         refs[2 * count + 2 * p + 1][...] = total.astype(BF16)
 
 
-def update_body(bits, share, scale, w_ref, *refs):
+def update_body(bits, share, scale, layer, at, w_ref, hot_ref, pre_ref, w_in_ref, *refs):
     count = len(bits)
-    nodes, table_ref = refs[2 * count : -1], refs[-1]
+    nodes, (table_ref, *outs) = refs[2 * count : -3], refs[-3:]
     totals = [refs[p][...] + swapped(refs[count + p], bit, share) for p, bit in enumerate(bits)]
     z = (jnp.concatenate(totals, axis=1) * scale).astype(BF16)
-    table_ref[...] = (joined(nodes).astype(F32) + silu(dot(z, w_ref[...]))).astype(BF16)
+    table = (joined(nodes).astype(F32) + silu(dot(z, w_ref[...]))).astype(BF16)
+    table_ref[...] = table
+    send_rows(layer, at, hot_ref, pre_ref, w_in_ref, table, outs)
 
 
 def order_body(order_ref, hot_ref, out):
@@ -125,14 +127,17 @@
     return (pre_ref[rows, :] + dot(h_rows, w)).astype(BF16)
 
 
-def send_body(layer, first, hot_ref, pre_ref, w_ref, table_ref, *outs):
+def send_rows(layer, first, hot_ref, pre_ref, w_ref, table, outs):
     block, width = outs[0].shape
-    table = table_ref[...]
     w = w_ref[layer, width : 2 * width, :]
     rows = [pl.ds((first + half) * block, block) for half in range(2)]
     h_rows = [dot(hot_ref[r, :], table).astype(BF16) for r in rows]
     for r, h, out in zip(rows, h_rows, outs):
         out[...] = (pre_ref[r, :] + dot(h, w)).astype(BF16)
+
+
+def send_body(layer, first, hot_ref, pre_ref, w_ref, table_ref, *outs):
+    send_rows(layer, first, hot_ref, pre_ref, w_ref, table_ref[...], outs)
 
 
 def edge_blocks(layer, got, m_blocks, w_ref):
@@ -298,21 +303,22 @@
             (order, *((m,) if first else [part for part, _ in m_parts]), w_in),
             PAIRS * product,
         )
-        (h,) = call(
-            functools.partial(update_body, bits, share, scale),
-            [sds(points, width, BF16)],
-            (w_node[layer], *sums[::2], *got, *table),
-            2 * points * width * width,
+        h, *outs = call(
+            functools.partial(update_body, bits, share, scale, layer, 4),
+            [sds(points, width, BF16)] + [sds(block, width, BF16)] * 2,
+            (w_node[layer], hot_sent, pre, w_in, *sums[::2], *got, *table),
+            2 * points * width * width + 2 * product,
         )
         table = [h]
         sent = {}
         for pair in (2, 1, 3):
-            outs = call(
-                functools.partial(send_body, layer, 2 * pair),
-                [sds(block, width, BF16)] * 2,
-                (hot_sent, pre, w_in, h),
-                2 * product,
-            )
+            if pair != 2:
+                outs = call(
+                    functools.partial(send_body, layer, 2 * pair),
+                    [sds(block, width, BF16)] * 2,
+                    (hot_sent, pre, w_in, h),
+                    2 * product,
+                )
             for half, out in enumerate(outs):
                 k = 2 * pair + half
                 sent[k ^ 1] = col_shift(out, OFFSETS[k])

time: 78.2 us -> 77.9 us (level)
  the two profiles are of different devices: /device:TPU:1 before, /device:TPU:0 now
where the time goes in v2:
time: 77.9 us; the launch traced here: 77.7 us
  starting transfers between devices  28.6 us (37%)
  waiting for transfers between devices  25 us (32%)
  Pallas kernels  19.7 us (25%)
  local copies, waits for them, and re-layouts  2.51 us (3%)
  between operations  1.06 us (1%)
  other arithmetic  0.94 us (1%)
    pallas_call x18, Pallas kernels, call(): pl.pallas_call(body, out_shape=tuple((jax.ShapeDtypeStruct(o.shape, o.dty...  19.7 us
    ppermute x12, starting transfers between devices, col_shift(): lax.ppermute(value, 'col', [(s, (s + steps) % count) for s in range(count)])  15.3 us
    ppermute x11, starting transfers between devices, row_move(): return lax.ppermute(value, 'row', [(s, s ^ bit) for s in range(count)])  13.3 us
    ppermute x12, waiting for transfers between devices, col_shift(): lax.ppermute(value, 'col', [(s, (s + steps) % count) for s in range(count)])  13.1 us
    ppermute x11, waiting for transfers between devices, row_move(): return lax.ppermute(value, 'row', [(s, s ^ bit) for s in range(count)])  11.9 us
  transfers between devices with their start and end apart: 23, of which 14 were waited for; matrix products, arithmetic and copies ran while one was open for 3% of the time, Pallas kernels for 18%

profile of v2, /device:TPU:0, one launch (start us, length us, event | category | flops | bytes accessed | tf_op | source)
XLA Modules:
  0.0 77.7 jit_solution(12880967047373167310)
XLA Ops:
  0.6 4.0 %collective-permute-start.6 = (bf16[64,512]{1,0:T(8,128)(2,1)}, bf16[64,512]{1,0:T(8,128)(2,1)S(1)}, u32[]{:S(2)}, u32[]{:S(2)}) collective-permute-start(bf16[64,512]{1,0:T(8,128)(2,1)} %bitcast.24), channel_id=1, source_target_pairs={{0,24},{8,16},{16,8},{24,0},{1,25},{9,17},{17,9},{25,1},{2,26},{10... | collective-permute-start | bytes 196616 | tf_op jit(solution)/shard_map/ppermute | solution.py:227
  4.6 0.5 collective-permute-start.5
  5.1 0.1 collective-permute-start.4
  5.3 0.7 fusion.1.targets_ref.refs_0_
  6.0 0.0 copy-start.2
  6.0 1.2 %copy-done.2 = bf16[1,1,1024,512]{3,2,1,0:T(8,128)(2,1)S(1)} copy-done((bf16[1,1,1024,512]{3,2,1,0:T(8,128)(2,1)S(1)}, bf16[1,1,1024,512]{3,2,1,0:T(8,128)(2,1)}, u32[]{:S(2)}) %copy-start.2) | copy-done | bytes 1048600
  7.2 0.5 shard_map.86
  7.7 0.0 copy-start
  7.7 2.0 %collective-permute-start = (bf16[256,256]{1,0:T(8,128)(2,1)S(1)}, bf16[256,256]{1,0:T(8,128)(2,1)S(1)}, u32[]{:S(2)}, u32[]{:S(2)}) collective-permute-start(bf16[256,256]{1,0:T(8,128)(2,1)S(1)} %get-tuple-element.60), channel_id=1, source_target_pairs={{0,8},{8,0},{16,24},{24,16},{1,9},{9,1},{17,25},{25,17},{2,10},{10... | collective-permute-start | bytes 393224 | tf_op jit(solution)/shard_map/ppermute | solution.py:227
  9.7 1.5 %collective-permute-start.1 = (bf16[256,256]{1,0:T(8,128)(2,1)S(1)}, bf16[256,256]{1,0:T(8,128)(2,1)S(1)}, u32[]{:S(2)}, u32[]{:S(2)}) collective-permute-start(bf16[256,256]{1,0:T(8,128)(2,1)S(1)} %get-tuple-element.61), channel_id=1, source_target_pairs={{0,16},{8,24},{16,0},{24,8},{1,17},{9,25},{17,1},{25,9},{2,18},{10... | collective-permute-start | bytes 393224 | tf_op jit(solution)/shard_map/ppermute | solution.py:227
  11.2 1.3 %slice_bitcast_fusion = (bf16[512,512]{1,0:T(8,128)(2,1)S(1)}, bf16[512,512]{1,0:T(8,128)(2,1)S(1)}) fusion(bf16[2,512,512]{2,1,0:T(8,128)(2,1)} %param.13), kind=kLoop, calls=%fused_computation.2 | loop fusion | bytes 2097152 | tf_op jit(solution)/shard_map/squeeze | solution.py:309
  12.5 0.3 collective-permute-done.refs_2_
  12.8 1.9 %collective-permute-done.1.refs_3_ = bf16[256,256]{1,0:T(8,128)(2,1)S(1)} collective-permute-done((bf16[256,256]{1,0:T(8,128)(2,1)S(1)}, bf16[256,256]{1,0:T(8,128)(2,1)S(1)}, u32[]{:S(2)}, u32[]{:S(2)}) %collective-permute-start.1) | collective-permute-done | bytes 131104 | tf_op jit(solution)/shard_map/ppermute | solution.py:227
  14.7 0.1 shard_map.89
  14.7 1.6 %collective-permute-start.2 = (bf16[256,256]{1,0:T(8,128)(2,1)S(1)}, bf16[256,256]{1,0:T(8,128)(2,1)S(1)}, u32[]{:S(2)}, u32[]{:S(2)}) collective-permute-start(bf16[256,256]{1,0:T(8,128)(2,1)S(1)} %get-tuple-element.64), channel_id=1, source_target_pairs={{0,16},{8,24},{16,0},{24,8},{1,17},{9,25},{17,1},{25,9},{2,18},{10... | collective-permute-start | bytes 393224 | tf_op jit(solution)/shard_map/ppermute | solution.py:227
  16.3 0.5 collective-permute-start.3
  16.9 0.2 fusion.hot_ref
  17.1 0.3 shard_map.87.hot_ref.sent_ref
  17.4 0.0 copy-start.3
  17.4 1.0 %shard_map.88.pre_ref = f32[1024,512]{1,0:T(8,128)S(1)} custom-call(s32[8,128]{1,0:T(8,128)S(1)} %bitcast.29, bf16[1024,512]{1,0:T(8,128)(2,1)S(1)} %get-tuple-element.55.refs_0_.m_ref, bf16[2,1536,512]{2,1,0:T(8,128)(2,1)S(1)} %copy-done), custom_call_target="tpu_custom_call" | custom-call | flops 536870912 | bytes 6295552 | tf_op jit(solution)/shard_map/pallas_call | solution.py:30
  18.4 0.0 collective-permute-done.6.refs_7_
  18.4 0.0 collective-permute-done.5.refs_6_
  18.4 1.4 %collective-permute-done.2.refs_2_ = bf16[256,256]{1,0:T(8,128)(2,1)S(1)} collective-permute-done((bf16[256,256]{1,0:T(8,128)(2,1)S(1)}, bf16[256,256]{1,0:T(8,128)(2,1)S(1)}, u32[]{:S(2)}, u32[]{:S(2)}) %collective-permute-start.2) | collective-permute-done | bytes 131104 | tf_op jit(solution)/shard_map/ppermute | solution.py:227
  19.8 1.5 %collective-permute-done.3.refs_3_ = bf16[256,256]{1,0:T(8,128)(2,1)S(1)} collective-permute-done((bf16[256,256]{1,0:T(8,128)(2,1)S(1)}, bf16[256,256]{1,0:T(8,128)(2,1)S(1)}, u32[]{:S(2)}, u32[]{:S(2)}) %collective-permute-start.3) | collective-permute-done | bytes 131104 | tf_op jit(solution)/shard_map/ppermute | solution.py:227
  21.3 0.8 %shard_map.90 = (bf16[256,512]{1,0:T(8,128)(2,1)S(1)}, bf16[128,512]{1,0:T(8,128)(2,1)S(1)}, bf16[128,512]{1,0:T(8,128)(2,1)S(1)}) custom-call(bf16[512,512]{1,0:T(8,128)(2,1)S(1)} %get-tuple-element.99.w_ref, bf16[1024,256]{1,0:T(8,128)(2,1)S(1)} %shard_map.87.hot_ref.sent_ref, f32[1024,512]{1,0:T(8,128)S(1)} %shard_map.88.pre_ref, ...), custom_call_target="tpu_custom_call" | custom-call | flops 402653184 | bytes 7864320 | tf_op jit(solution)/shard_map/pallas_call | solution.py:30
  22.1 0.4 shard_map.94
  22.5 0.0 copy-start.1
  22.6 0.4 shard_map.92
  23.0 3.7 %collective-permute-start.9 = (bf16[128,512]{1,0:T(8,128)(2,1)S(1)}, bf16[128,512]{1,0:T(8,128)(2,1)S(1)}, u32[]{:S(2)}, u32[]{:S(2)}) collective-permute-start(bf16[128,512]{1,0:T(8,128)(2,1)S(1)} %get-tuple-element.73), channel_id=1, source_target_pairs={{0,6},{1,7},{2,0},{3,1},{4,2},{5,3},{6,4},{7,5},{8,14},{9,15},{10,... | collective-permute-start | bytes 393224 | tf_op jit(solution)/shard_map/ppermute | solution.py:232
  26.7 0.0 collective-permute-start.11
  26.7 2.2 %collective-permute-start.7 = (bf16[128,512]{1,0:T(8,128)(2,1)S(1)}, bf16[128,512]{1,0:T(8,128)(2,1)S(1)}, u32[]{:S(2)}, u32[]{:S(2)}) collective-permute-start(bf16[128,512]{1,0:T(8,128)(2,1)S(1)} %get-tuple-element.71), channel_id=1, source_target_pairs={{0,7},{1,0},{2,1},{3,2},{4,3},{5,4},{6,5},{7,6},{8,15},{9,8},{10,9... | collective-permute-start | bytes 393224 | tf_op jit(solution)/shard_map/ppermute | solution.py:232
  28.9 1.7 %collective-permute-start.8 = (bf16[128,512]{1,0:T(8,128)(2,1)S(1)}, bf16[128,512]{1,0:T(8,128)(2,1)S(1)}, u32[]{:S(2)}, u32[]{:S(2)}) collective-permute-start(bf16[128,512]{1,0:T(8,128)(2,1)S(1)} %get-tuple-element.72), channel_id=1, source_target_pairs={{0,1},{1,2},{2,3},{3,4},{4,5},{5,6},{6,7},{7,0},{8,9},{9,10},{10,1... | collective-permute-start | bytes 393224 | tf_op jit(solution)/shard_map/ppermute | solution.py:232
  30.6 2.4 %shard_map.91 = (f32[768,512]{1,0:T(8,128)S(1)}, bf16[256,512]{1,0:T(8,128)(2,1)S(1)}, f32[256,512]{1,0:T(8,128)S(1)}) custom-call(bf16[1024,256]{1,0:T(8,128)(2,1)S(1)} %fusion.hot_ref, bf16[1024,256]{1,0:T(8,128)(2,1)S(1)} %shard_map.87.hot_ref.sent_ref, f32[1024,512]{1,0:T(8,128)S(1)} %shard_map.88.pre_ref, ...), custom_call_target="tpu_custom_call" | custom-call | flops 1610612736 | bytes 14159872 | tf_op jit(solution)/shard_map/pallas_call | solution.py:30
  33.0 0.1 collective-permute-start.12
  33.1 0.4 collective-permute-done.10.refs_3_
  33.5 2.3 %collective-permute-done.7.refs_0_ = bf16[128,512]{1,0:T(8,128)(2,1)S(1)} collective-permute-done((bf16[128,512]{1,0:T(8,128)(2,1)S(1)}, bf16[128,512]{1,0:T(8,128)(2,1)S(1)}, u32[]{:S(2)}, u32[]{:S(2)}) %collective-permute-start.7) | collective-permute-done | bytes 131104 | tf_op jit(solution)/shard_map/ppermute | solution.py:232
  35.9 0.7 collective-permute-done.8.refs_1_
  36.5 2.2 %shard_map.93 = (bf16[512,512]{1,0:T(8,128)(2,1)S(1)}, f32[256,512]{1,0:T(8,128)S(1)}) custom-call(f32[768,512]{1,0:T(8,128)S(1)} %get-tuple-element.69.part_ref, bf16[1024,512]{1,0:T(8,128)(2,1)S(1)} %get-tuple-element.55.refs_0_.m_ref, bf16[2,2,2,512,512]{4,3,2,1,0:T(8,128)(2,1)S(1)} %copy-done.1, s32[1,1024]{1,0:T(1,128)S(1)} %fusion.1.targets_ref.refs_0_, ...), custom_call_target="tpu_custom_call" | custom-call | flops 1610612736 | bytes 8916992 | tf_op jit(solution)/shard_map/pallas_call | solution.py:30
  38.8 3.8 %collective-permute-done.12.refs_1_ = bf16[128,512]{1,0:T(8,128)(2,1)S(1)} collective-permute-done((bf16[128,512]{1,0:T(8,128)(2,1)S(1)}, bf16[128,512]{1,0:T(8,128)(2,1)S(1)}, u32[]{:S(2)}, u32[]{:S(2)}) %collective-permute-start.12) | collective-permute-done | bytes 131104 | tf_op jit(solution)/shard_map/ppermute | solution.py:232
  42.6 1.4 %shard_map.95 = (bf16[256,512]{1,0:T(8,128)(2,1)S(1)}, f32[256,256]{1,0:T(8,128)S(1)}, bf16[256,256]{1,0:T(8,128)(2,1)S(1)}, f32[256,256]{1,0:T(8,128)S(1)}, bf16[256,256]{1,0:T(8,128)(2,1)S(1)}) custom-call(f32[768,512]{1,0:T(8,128)S(1)} %get-tuple-element.69.part_ref, bf16[1024,512]{1,0:T(8,128)(2,1)S(1)} %get-tuple-element.55.refs_0_.m_ref, ...), custom_call_target="tpu_custom_call" | custom-call | flops 805306368 | bytes 8654848 | tf_op jit(solution)/shard_map/pallas_call | solution.py:30
  43.9 0.4 collective-permute-start.13
  44.4 0.5 collective-permute-start.14
  44.9 4.1 %collective-permute-done.13.refs_2_ = bf16[256,256]{1,0:T(8,128)(2,1)S(1)} collective-permute-done((bf16[256,256]{1,0:T(8,128)(2,1)S(1)}, bf16[256,256]{1,0:T(8,128)(2,1)S(1)}, u32[]{:S(2)}, u32[]{:S(2)}) %collective-permute-start.13) | collective-permute-done | bytes 131104 | tf_op jit(solution)/shard_map/ppermute | solution.py:227
  49.0 0.4 collective-permute-done.14.refs_3_
  49.4 0.1 shard_map.97
  49.5 0.6 collective-permute-start.15
  50.0 1.6 %collective-permute-start.16 = (bf16[256,256]{1,0:T(8,128)(2,1)S(1)}, bf16[256,256]{1,0:T(8,128)(2,1)S(1)}, u32[]{:S(2)}, u32[]{:S(2)}) collective-permute-start(bf16[256,256]{1,0:T(8,128)(2,1)S(1)} %get-tuple-element.87), channel_id=1, source_target_pairs={{0,8},{8,0},{16,24},{24,16},{1,9},{9,1},{17,25},{25,17},{2,10},{10... | collective-permute-start | bytes 393224 | tf_op jit(solution)/shard_map/ppermute | solution.py:227
  51.7 1.1 %shard_map.96.pre_ref = f32[1024,512]{1,0:T(8,128)S(1)} custom-call(s32[8,128]{1,0:T(8,128)S(1)} %bitcast.30, bf16[256,512]{1,0:T(8,128)(2,1)S(1)} %get-tuple-element.68.refs_0_.m_ref, bf16[512,512]{1,0:T(8,128)(2,1)S(1)} %get-tuple-element.75.refs_1_.m_ref, bf16[256,512]{1,0:T(8,128)(2,1)S(1)} %get-tuple-element.79.refs_2_.m_ref, ...), custom_call_target="tpu_custom_call" | custom-call | flops 536870912 | bytes 6295552 | tf_op jit(solution)/shard_map/pallas_call | solution.py:30
  52.8 1.8 %collective-permute-done.15.refs_2_ = bf16[256,256]{1,0:T(8,128)(2,1)S(1)} collective-permute-done((bf16[256,256]{1,0:T(8,128)(2,1)S(1)}, bf16[256,256]{1,0:T(8,128)(2,1)S(1)}, u32[]{:S(2)}, u32[]{:S(2)}) %collective-permute-start.15) | collective-permute-done | bytes 131104 | tf_op jit(solution)/shard_map/ppermute | solution.py:227
  54.5 0.5 collective-permute-done.16.refs_3_
  55.0 0.8 %shard_map.98 = (bf16[256,512]{1,0:T(8,128)(2,1)S(1)}, bf16[128,512]{1,0:T(8,128)(2,1)S(1)}, bf16[128,512]{1,0:T(8,128)(2,1)S(1)}) custom-call(bf16[512,512]{1,0:T(8,128)(2,1)S(1)} %get-tuple-element.98.w_ref, bf16[1024,256]{1,0:T(8,128)(2,1)S(1)} %shard_map.87.hot_ref.sent_ref, f32[1024,512]{1,0:T(8,128)S(1)} %shard_map.96.pre_ref, ...), custom_call_target="tpu_custom_call" | custom-call | flops 402653184 | bytes 7864320 | tf_op jit(solution)/shard_map/pallas_call | solution.py:30
  55.8 3.3 %collective-permute-start.21 = (bf16[128,512]{1,0:T(8,128)(2,1)S(1)}, bf16[128,512]{1,0:T(8,128)(2,1)S(1)}, u32[]{:S(2)}, u32[]{:S(2)}) collective-permute-start(bf16[128,512]{1,0:T(8,128)(2,1)S(1)} %get-tuple-element.94), channel_id=1, source_target_pairs={{0,6},{1,7},{2,0},{3,1},{4,2},{5,3},{6,4},{7,5},{8,14},{9,15},{10,... | collective-permute-start | bytes 393224 | tf_op jit(solution)/shard_map/ppermute | solution.py:232
  59.2 0.0 collective-permute-start.22
  59.2 0.4 shard_map.101
  59.6 0.1 collective-permute-start.19
  59.7 0.5 collective-permute-start.20
  60.2 0.4 shard_map.100
  60.6 3.7 %collective-permute-start.17 = (bf16[128,512]{1,0:T(8,128)(2,1)S(1)}, bf16[128,512]{1,0:T(8,128)(2,1)S(1)}, u32[]{:S(2)}, u32[]{:S(2)}) collective-permute-start(bf16[128,512]{1,0:T(8,128)(2,1)S(1)} %get-tuple-element.90), channel_id=1, source_target_pairs={{0,5},{1,6},{2,7},{3,0},{4,1},{5,2},{6,3},{7,4},{8,13},{9,14},{10,... | collective-permute-start | bytes 393224 | tf_op jit(solution)/shard_map/ppermute | solution.py:232
  64.3 0.0 collective-permute-start.18
  64.3 2.9 %shard_map.99 = (f32[768,512]{1,0:T(8,128)S(1)}, bf16[256,512]{1,0:T(8,128)(2,1)S(1)}, bf16[64,512]{1,0:T(8,128)(2,1)}) custom-call(bf16[1024,256]{1,0:T(8,128)(2,1)S(1)} %fusion.hot_ref, bf16[1024,256]{1,0:T(8,128)(2,1)S(1)} %shard_map.87.hot_ref.sent_ref, f32[1024,512]{1,0:T(8,128)S(1)} %shard_map.96.pre_ref, ...), custom_call_target="tpu_custom_call" | custom-call | flops 1610612736 | bytes 12910592 | tf_op jit(solution)/shard_map/pallas_call | solution.py:30
  67.2 0.5 collective-permute-done.20.refs_1_
  67.7 2.7 %shard_map.102.refs_2_ = bf16[1024,512]{1,0:T(8,128)(2,1)} custom-call(f32[768,512]{1,0:T(8,128)S(1)} %get-tuple-element.89.part_ref, bf16[512,512]{1,0:T(8,128)(2,1)S(1)} %get-tuple-element.75.refs_1_.m_ref, bf16[2,2,2,512,512]{4,3,2,1,0:T(8,128)(2,1)S(1)} %copy-done.1, bf16[128,512]{1,0:T(8,128)(2,1)S(1)} %collective-permute-done.19.refs_0_, ...), custom_call_target="tpu_custom_call" | custom-call | flops 1073741824 | bytes 8126464 | tf_op jit(solution)/shard_map/pallas_call | solution.py:30
  70.4 5.4 %collective-permute-done.18.refs_1_ = bf16[128,512]{1,0:T(8,128)(2,1)S(1)} collective-permute-done((bf16[128,512]{1,0:T(8,128)(2,1)S(1)}, bf16[128,512]{1,0:T(8,128)(2,1)S(1)}, u32[]{:S(2)}, u32[]{:S(2)}) %collective-permute-start.18) | collective-permute-done | bytes 131104 | tf_op jit(solution)/shard_map/ppermute | solution.py:232
  75.8 1.8 %shard_map.103 = bf16[1024,512]{1,0:T(8,128)(2,1)} custom-call(f32[768,512]{1,0:T(8,128)S(1)} %get-tuple-element.89.part_ref, bf16[256,512]{1,0:T(8,128)(2,1)S(1)} %get-tuple-element.79.refs_2_.m_ref, bf16[2,2,2,512,512]{4,3,2,1,0:T(8,128)(2,1)S(1)} %copy-done.1, ...), custom_call_target="tpu_custom_call", output_to_operand_aliasing={{}: (5, {})} | custom-call | flops 536870912 | bytes 8388608 | tf_op jit(solution)/shard_map/pallas_call | solution.py:30
  (16 shorter events, 0.1 us)
Async XLA Ops:
  0.6 11.9 %copy-start.5 = (s32[1,1,1024]{2,1,0:T(1,128)S(1)}, s32[1,1,1024]{2,1,0:T(1,128)}, u32[]{:S(2)}) copy-start(s32[1,1,1024]{2,1,0:T(1,128)} %param.8) | copy-start | bytes 12292
  0.6 17.7 %collective-permute-start.6 = (bf16[64,512]{1,0:T(8,128)(2,1)}, bf16[64,512]{1,0:T(8,128)(2,1)S(1)}, u32[]{:S(2)}, u32[]{:S(2)}) collective-permute-start(bf16[64,512]{1,0:T(8,128)(2,1)} %bitcast.24), channel_id=1, source_target_pairs={{0,24},{8,16},{16,8},{24,0},{1,25},{9,17},{17,9},{25,1},{2,26},{10... | collective-permute-start | bytes 196616 | tf_op jit(solution)/shard_map/ppermute | solution.py:227
  4.6 13.7 %collective-permute-start.5 = (bf16[64,512]{1,0:T(8,128)(2,1)}, bf16[64,512]{1,0:T(8,128)(2,1)S(1)}, u32[]{:S(2)}, u32[]{:S(2)}) collective-permute-start(bf16[64,512]{1,0:T(8,128)(2,1)} %bitcast.25), channel_id=1, source_target_pairs={{0,16},{8,24},{16,0},{24,8},{1,17},{9,25},{17,1},{25,9},{2,18},{10... | collective-permute-start | bytes 196616 | tf_op jit(solution)/shard_map/ppermute | solution.py:227
  5.1 13.2 %collective-permute-start.4 = (bf16[64,512]{1,0:T(8,128)(2,1)}, bf16[64,512]{1,0:T(8,128)(2,1)S(1)}, u32[]{:S(2)}, u32[]{:S(2)}) collective-permute-start(bf16[64,512]{1,0:T(8,128)(2,1)} %bitcast.26), channel_id=1, source_target_pairs={{0,8},{8,0},{16,24},{24,16},{1,9},{9,1},{17,25},{25,17},{2,10},{10... | collective-permute-start | bytes 196616 | tf_op jit(solution)/shard_map/ppermute | solution.py:227
  6.0 1.2 %copy-start.2 = (bf16[1,1,1024,512]{3,2,1,0:T(8,128)(2,1)S(1)}, bf16[1,1,1024,512]{3,2,1,0:T(8,128)(2,1)}, u32[]{:S(2)}) copy-start(bf16[1,1,1024,512]{3,2,1,0:T(8,128)(2,1)} %param.7) | copy-start | bytes 3145732
  7.2 9.8 %copy-start.4 = (s32[1,1,8,128]{3,2,1,0:T(8,128)S(1)}, s32[1,1,8,128]{3,2,1,0:T(8,128)}, u32[]{:S(2)}) copy-start(s32[1,1,8,128]{3,2,1,0:T(8,128)} %param.9) | copy-start | bytes 12292
  7.7 9.6 %copy-start = (bf16[2,1536,512]{2,1,0:T(8,128)(2,1)S(1)}, bf16[2,1536,512]{2,1,0:T(8,128)(2,1)}, u32[]{:S(2)}) copy-start(bf16[2,1536,512]{2,1,0:T(8,128)(2,1)} %w_ref.7) | copy-start | bytes 9437188
  7.7 5.0 %collective-permute-start = (bf16[256,256]{1,0:T(8,128)(2,1)S(1)}, bf16[256,256]{1,0:T(8,128)(2,1)S(1)}, u32[]{:S(2)}, u32[]{:S(2)}) collective-permute-start(bf16[256,256]{1,0:T(8,128)(2,1)S(1)} %get-tuple-element.60), channel_id=1, source_target_pairs={{0,8},{8,0},{16,24},{24,16},{1,9},{9,1},{17,25},{25,17},{2,10},{10... | collective-permute-start | bytes 393224 | tf_op jit(solution)/shard_map/ppermute | solution.py:227
  9.7 5.0 %collective-permute-start.1 = (bf16[256,256]{1,0:T(8,128)(2,1)S(1)}, bf16[256,256]{1,0:T(8,128)(2,1)S(1)}, u32[]{:S(2)}, u32[]{:S(2)}) collective-permute-start(bf16[256,256]{1,0:T(8,128)(2,1)S(1)} %get-tuple-element.61), channel_id=1, source_target_pairs={{0,16},{8,24},{16,0},{24,8},{1,17},{9,25},{17,1},{25,9},{2,18},{10... | collective-permute-start | bytes 393224 | tf_op jit(solution)/shard_map/ppermute | solution.py:227
  14.7 5.0 %collective-permute-start.2 = (bf16[256,256]{1,0:T(8,128)(2,1)S(1)}, bf16[256,256]{1,0:T(8,128)(2,1)S(1)}, u32[]{:S(2)}, u32[]{:S(2)}) collective-permute-start(bf16[256,256]{1,0:T(8,128)(2,1)S(1)} %get-tuple-element.64), channel_id=1, source_target_pairs={{0,16},{8,24},{16,0},{24,8},{1,17},{9,25},{17,1},{25,9},{2,18},{10... | collective-permute-start | bytes 393224 | tf_op jit(solution)/shard_map/ppermute | solution.py:227
  16.3 5.0 %collective-permute-start.3 = (bf16[256,256]{1,0:T(8,128)(2,1)S(1)}, bf16[256,256]{1,0:T(8,128)(2,1)S(1)}, u32[]{:S(2)}, u32[]{:S(2)}) collective-permute-start(bf16[256,256]{1,0:T(8,128)(2,1)S(1)} %get-tuple-element.65), channel_id=1, source_target_pairs={{0,8},{8,0},{16,24},{24,16},{1,9},{9,1},{17,25},{25,17},{2,10},{10... | collective-permute-start | bytes 393224 | tf_op jit(solution)/shard_map/ppermute | solution.py:227
  17.4 3.9 %copy-start.3 = (bf16[1,64,512]{2,1,0:T(8,128)(2,1)S(1)}, bf16[1,64,512]{2,1,0:T(8,128)(2,1)}, u32[]{:S(2)}) copy-start(bf16[1,64,512]{2,1,0:T(8,128)(2,1)} %param.10) | copy-start | bytes 196612
  22.5 8.1 %copy-start.1 = (bf16[2,2,2,512,512]{4,3,2,1,0:T(8,128)(2,1)S(1)}, bf16[2,2,2,512,512]{4,3,2,1,0:T(8,128)(2,1)}, u32[]{:S(2)}) copy-start(bf16[2,2,2,512,512]{4,3,2,1,0:T(8,128)(2,1)} %w_ref.9) | copy-start | bytes 12582916
  23.0 10.0 %collective-permute-start.9 = (bf16[128,512]{1,0:T(8,128)(2,1)S(1)}, bf16[128,512]{1,0:T(8,128)(2,1)S(1)}, u32[]{:S(2)}, u32[]{:S(2)}) collective-permute-start(bf16[128,512]{1,0:T(8,128)(2,1)S(1)} %get-tuple-element.73), channel_id=1, source_target_pairs={{0,6},{1,7},{2,0},{3,1},{4,2},{5,3},{6,4},{7,5},{8,14},{9,15},{10,... | collective-permute-start | bytes 393224 | tf_op jit(solution)/shard_map/ppermute | solution.py:232
  26.7 6.9 %collective-permute-start.10 = (bf16[128,512]{1,0:T(8,128)(2,1)S(1)}, bf16[128,512]{1,0:T(8,128)(2,1)S(1)}, u32[]{:S(2)}, u32[]{:S(2)}) collective-permute-start(bf16[128,512]{1,0:T(8,128)(2,1)S(1)} %get-tuple-element.74), channel_id=1, source_target_pairs={{0,2},{1,3},{2,4},{3,5},{4,6},{5,7},{6,0},{7,1},{8,10},{9,11},{10,... | collective-permute-start | bytes 393224 | tf_op jit(solution)/shard_map/ppermute | solution.py:232
  26.7 12.1 %collective-permute-start.11 = (bf16[128,512]{1,0:T(8,128)(2,1)S(1)}, bf16[128,512]{1,0:T(8,128)(2,1)S(1)}, u32[]{:S(2)}, u32[]{:S(2)}) collective-permute-start(bf16[128,512]{1,0:T(8,128)(2,1)S(1)} %get-tuple-element.77), channel_id=1, source_target_pairs={{0,5},{1,6},{2,7},{3,0},{4,1},{5,2},{6,3},{7,4},{8,13},{9,14},{10,... | collective-permute-start | bytes 393224 | tf_op jit(solution)/shard_map/ppermute | solution.py:232
  26.7 9.2 %collective-permute-start.7 = (bf16[128,512]{1,0:T(8,128)(2,1)S(1)}, bf16[128,512]{1,0:T(8,128)(2,1)S(1)}, u32[]{:S(2)}, u32[]{:S(2)}) collective-permute-start(bf16[128,512]{1,0:T(8,128)(2,1)S(1)} %get-tuple-element.71), channel_id=1, source_target_pairs={{0,7},{1,0},{2,1},{3,2},{4,3},{5,4},{6,5},{7,6},{8,15},{9,8},{10,9... | collective-permute-start | bytes 393224 | tf_op jit(solution)/shard_map/ppermute | solution.py:232
  28.9 7.7 %collective-permute-start.8 = (bf16[128,512]{1,0:T(8,128)(2,1)S(1)}, bf16[128,512]{1,0:T(8,128)(2,1)S(1)}, u32[]{:S(2)}, u32[]{:S(2)}) collective-permute-start(bf16[128,512]{1,0:T(8,128)(2,1)S(1)} %get-tuple-element.72), channel_id=1, source_target_pairs={{0,1},{1,2},{2,3},{3,4},{4,5},{5,6},{6,7},{7,0},{8,9},{9,10},{10,1... | collective-permute-start | bytes 393224 | tf_op jit(solution)/shard_map/ppermute | solution.py:232
  33.0 9.6 %collective-permute-start.12 = (bf16[128,512]{1,0:T(8,128)(2,1)S(1)}, bf16[128,512]{1,0:T(8,128)(2,1)S(1)}, u32[]{:S(2)}, u32[]{:S(2)}) collective-permute-start(bf16[128,512]{1,0:T(8,128)(2,1)S(1)} %get-tuple-element.78), channel_id=1, source_target_pairs={{0,3},{1,4},{2,5},{3,6},{4,7},{5,0},{6,1},{7,2},{8,11},{9,12},{10,... | collective-permute-start | bytes 393224 | tf_op jit(solution)/shard_map/ppermute | solution.py:232
  43.9 5.0 %collective-permute-start.13 = (bf16[256,256]{1,0:T(8,128)(2,1)S(1)}, bf16[256,256]{1,0:T(8,128)(2,1)S(1)}, u32[]{:S(2)}, u32[]{:S(2)}) collective-permute-start(bf16[256,256]{1,0:T(8,128)(2,1)S(1)} %get-tuple-element.82), channel_id=1, source_target_pairs={{0,8},{8,0},{16,24},{24,16},{1,9},{9,1},{17,25},{25,17},{2,10},{10... | collective-permute-start | bytes 393224 | tf_op jit(solution)/shard_map/ppermute | solution.py:227
  44.4 5.1 %collective-permute-start.14 = (bf16[256,256]{1,0:T(8,128)(2,1)S(1)}, bf16[256,256]{1,0:T(8,128)(2,1)S(1)}, u32[]{:S(2)}, u32[]{:S(2)}) collective-permute-start(bf16[256,256]{1,0:T(8,128)(2,1)S(1)} %get-tuple-element.83), channel_id=1, source_target_pairs={{0,16},{8,24},{16,0},{24,8},{1,17},{9,25},{17,1},{25,9},{2,18},{10... | collective-permute-start | bytes 393224 | tf_op jit(solution)/shard_map/ppermute | solution.py:227
  49.5 5.0 %collective-permute-start.15 = (bf16[256,256]{1,0:T(8,128)(2,1)S(1)}, bf16[256,256]{1,0:T(8,128)(2,1)S(1)}, u32[]{:S(2)}, u32[]{:S(2)}) collective-permute-start(bf16[256,256]{1,0:T(8,128)(2,1)S(1)} %get-tuple-element.86), channel_id=1, source_target_pairs={{0,16},{8,24},{16,0},{24,8},{1,17},{9,25},{17,1},{25,9},{2,18},{10... | collective-permute-start | bytes 393224 | tf_op jit(solution)/shard_map/ppermute | solution.py:227
  50.0 5.0 %collective-permute-start.16 = (bf16[256,256]{1,0:T(8,128)(2,1)S(1)}, bf16[256,256]{1,0:T(8,128)(2,1)S(1)}, u32[]{:S(2)}, u32[]{:S(2)}) collective-permute-start(bf16[256,256]{1,0:T(8,128)(2,1)S(1)} %get-tuple-element.87), channel_id=1, source_target_pairs={{0,8},{8,0},{16,24},{24,16},{1,9},{9,1},{17,25},{25,17},{2,10},{10... | collective-permute-start | bytes 393224 | tf_op jit(solution)/shard_map/ppermute | solution.py:227
  55.8 8.5 %collective-permute-start.21 = (bf16[128,512]{1,0:T(8,128)(2,1)S(1)}, bf16[128,512]{1,0:T(8,128)(2,1)S(1)}, u32[]{:S(2)}, u32[]{:S(2)}) collective-permute-start(bf16[128,512]{1,0:T(8,128)(2,1)S(1)} %get-tuple-element.94), channel_id=1, source_target_pairs={{0,6},{1,7},{2,0},{3,1},{4,2},{5,3},{6,4},{7,5},{8,14},{9,15},{10,... | collective-permute-start | bytes 393224 | tf_op jit(solution)/shard_map/ppermute | solution.py:232
  59.2 8.1 %collective-permute-start.22 = (bf16[128,512]{1,0:T(8,128)(2,1)S(1)}, bf16[128,512]{1,0:T(8,128)(2,1)S(1)}, u32[]{:S(2)}, u32[]{:S(2)}) collective-permute-start(bf16[128,512]{1,0:T(8,128)(2,1)S(1)} %get-tuple-element.95), channel_id=1, source_target_pairs={{0,2},{1,3},{2,4},{3,5},{4,6},{5,7},{6,0},{7,1},{8,10},{9,11},{10,... | collective-permute-start | bytes 393224 | tf_op jit(solution)/shard_map/ppermute | solution.py:232
  59.6 7.6 %collective-permute-start.19 = (bf16[128,512]{1,0:T(8,128)(2,1)S(1)}, bf16[128,512]{1,0:T(8,128)(2,1)S(1)}, u32[]{:S(2)}, u32[]{:S(2)}) collective-permute-start(bf16[128,512]{1,0:T(8,128)(2,1)S(1)} %get-tuple-element.92), channel_id=1, source_target_pairs={{0,7},{1,0},{2,1},{3,2},{4,3},{5,4},{6,5},{7,6},{8,15},{9,8},{10,9... | collective-permute-start | bytes 393224 | tf_op jit(solution)/shard_map/ppermute | solution.py:232
  59.7 8.1 %collective-permute-start.20 = (bf16[128,512]{1,0:T(8,128)(2,1)S(1)}, bf16[128,512]{1,0:T(8,128)(2,1)S(1)}, u32[]{:S(2)}, u32[]{:S(2)}) collective-permute-start(bf16[128,512]{1,0:T(8,128)(2,1)S(1)} %get-tuple-element.93), channel_id=1, source_target_pairs={{0,1},{1,2},{2,3},{3,4},{4,5},{5,6},{6,7},{7,0},{8,9},{9,10},{10,1... | collective-permute-start | bytes 393224 | tf_op jit(solution)/shard_map/ppermute | solution.py:232
  60.6 9.8 %collective-permute-start.17 = (bf16[128,512]{1,0:T(8,128)(2,1)S(1)}, bf16[128,512]{1,0:T(8,128)(2,1)S(1)}, u32[]{:S(2)}, u32[]{:S(2)}) collective-permute-start(bf16[128,512]{1,0:T(8,128)(2,1)S(1)} %get-tuple-element.90), channel_id=1, source_target_pairs={{0,5},{1,6},{2,7},{3,0},{4,1},{5,2},{6,3},{7,4},{8,13},{9,14},{10,... | collective-permute-start | bytes 393224 | tf_op jit(solution)/shard_map/ppermute | solution.py:232
  64.3 11.5 %collective-permute-start.18 = (bf16[128,512]{1,0:T(8,128)(2,1)S(1)}, bf16[128,512]{1,0:T(8,128)(2,1)S(1)}, u32[]{:S(2)}, u32[]{:S(2)}) collective-permute-start(bf16[128,512]{1,0:T(8,128)(2,1)S(1)} %get-tuple-element.91), channel_id=1, source_target_pairs={{0,3},{1,4},{2,5},{3,6},{4,7},{5,0},{6,1},{7,2},{8,11},{9,12},{10,... | collective-permute-start | bytes 393224 | tf_op jit(solution)/shard_map/ppermute | solution.py:232
